TPU v7x, 32 devices: a whole 2x2x4 slice. The times are simulated.
32 devices in a mesh: row: 4 (over y, core), col: 8 (over z, x).
Axes of the slice: x: 2, y: 2, z: 4, core: 2. Of those that a mesh axis runs over, the one named last changes fastest.
Arguments:
- positions: float32 [3, 8192], P(None, 'col'), may hold values from 0 to 4
- modulus: float32 [8192], P('col'), may hold values from 0.5 to 2
- self_weight: float32 [64, 768], P('col'), may hold values from 1 to 4
- omega: float32 [64, 768, 256], P('col'), may hold values from -6 to 6
- psi: float32 [64, 768, 256], P('row'), may hold values from -6 to 6
- blocks: int32 [4, 8, 2, 2], P('row', 'col'), may hold values from -1 to 15, as said below
Outputs:
- row_basis: float32 [64, 768, 256], P('row', 'col')
- col_basis: float32 [64, 768, 256], P('col', 'row')
Inputs may be any that keep to these rules, and one draw needn't show every extreme that they name: `blocks`: on every device the valid slots come first and the rest hold -1 in both entries; valid pairs are distinct, a row entry below 16, a column entry below 8, and never a cluster paired with itself; each device has at least one valid slot and some device has all 2 slots valid.
All inputs are finite; a program needn't handle non-finite values.
Results may differ from a plain program's by a relative error of at most 0.0003.
Values sent between devices are 32-bit elements; how exact they have to be, the bound alone decides.
A program may use at most 192 MiB of HBM per device.

v0:
```python
import jax
import jax.numpy as jnp
from jax import lax
from jax.sharding import PartitionSpec as P

COUPLE = 0.25
ROOT_TWO = 1.4142135623730951
HIGH = lax.Precision.HIGHEST
GROUP_SIZE = 2


def make_tiles(row_points, row_scale, col_points, col_scale):
    offsets = row_points[:, :, :, None] - col_points[:, :, None, :]
    spread = jnp.sum(offsets * offsets, axis=1) + 1.0
    inverse = lax.rsqrt(spread)
    normal = offsets * inverse[:, None]
    weight_ab = COUPLE * inverse * inverse * inverse * row_scale[:, :, None] * col_scale[:, None, :]
    comp_x = normal[:, 0]
    comp_y = normal[:, 1]
    comp_z = normal[:, 2]
    voigt = jnp.stack(
        [
            comp_x * comp_x,
            comp_y * comp_y,
            comp_z * comp_z,
            ROOT_TWO * comp_y * comp_z,
            ROOT_TWO * comp_x * comp_z,
            ROOT_TWO * comp_x * comp_y,
        ],
        axis=1,
    )
    trace_vec = jnp.array([1.0, 1.0, 1.0, 0.0, 0.0, 0.0], dtype=voigt.dtype)
    identity = jnp.eye(6, dtype=voigt.dtype)
    voigt_row = voigt[:, :, :, None, :]
    voigt_col = jnp.transpose(voigt, (0, 2, 1, 3))[:, None]
    angular = (
        identity[None, :, None, :, None]
        + voigt_row * trace_vec[None, None, None, :, None]
        + trace_vec[None, :, None, None, None] * voigt_col
        - 5.0 * voigt_row * voigt_col
    )
    result = angular * weight_ab[:, None, :, None, :]
    zones_per = row_points.shape[2]
    return result.reshape(result.shape[0], 6 * zones_per, 6 * zones_per)


def gram_of(sketch):
    return jnp.einsum("kxs,kxt->kst", sketch, sketch, precision=HIGH)


def apply_factor(gram, sketch):
    factor = jnp.linalg.cholesky(gram)
    return lax.linalg.triangular_solve(
        factor, sketch, left_side=False, lower=True, transpose_a=True
    )


def per_device(positions, modulus, self_weight, omega, psi, blocks):
    col_clusters = omega.shape[0]
    row_clusters = psi.shape[0]
    zones_per = positions.shape[1] // col_clusters
    height = omega.shape[1]
    width = omega.shape[2]
    all_points, all_scales = (
        lax.all_gather(positions, "col", axis=1, tiled=True),
        lax.all_gather(modulus, "col", axis=0, tiled=True),
    )
    row_index = lax.axis_index("row")
    col_index = lax.axis_index("col")
    row_points = lax.dynamic_slice_in_dim(
        all_points, row_index * row_clusters * zones_per, row_clusters * zones_per, 1
    ).reshape(3, row_clusters, zones_per)
    row_scales = lax.dynamic_slice_in_dim(
        all_scales, row_index * row_clusters * zones_per, row_clusters * zones_per, 0
    ).reshape(row_clusters, zones_per)
    col_points = positions.reshape(3, col_clusters, zones_per)
    col_scales = modulus.reshape(col_clusters, zones_per)
    on_diagonal = col_index * col_clusters // row_clusters == row_index
    offset_rows = jnp.clip(
        col_index * col_clusters - row_index * row_clusters, 0, row_clusters - col_clusters
    )
    own_rows = jnp.where(on_diagonal, self_weight[:, :, None] * omega, 0.0)
    row_sketch = lax.dynamic_update_slice_in_dim(
        jnp.zeros((row_clusters, height, width), jnp.float32), own_rows, offset_rows, 0
    )
    psi_local = lax.dynamic_slice_in_dim(psi, offset_rows, col_clusters, 0)
    col_sketch = jnp.where(on_diagonal, self_weight[:, :, None] * psi_local, 0.0)
    pair_list = blocks.reshape(-1, 2)
    slot_total = pair_list.shape[0]
    padded_count = (slot_total + GROUP_SIZE - 1) // GROUP_SIZE * GROUP_SIZE
    pair_list = jnp.concatenate(
        [pair_list, jnp.full((padded_count - slot_total, 2), -1, jnp.int32)], axis=0
    )
    live_count = jnp.sum((pair_list[:, 0] >= 0).astype(jnp.int32))
    group_count = (live_count + GROUP_SIZE - 1) // GROUP_SIZE

    def step(group_index, state):
        sketch_rows, sketch_cols = state
        live = (pair_list[:, 0] >= 0).astype(jnp.float32)
        row_ids = jnp.maximum(pair_list[:, 0], 0)
        col_ids = jnp.maximum(pair_list[:, 1], 0)
        left_points = jnp.transpose(row_points[:, row_ids], (1, 0, 2))
        right_points = jnp.transpose(col_points[:, col_ids], (1, 0, 2))
        blocks_now = (
            make_tiles(left_points, row_scales[row_ids], right_points, col_scales[col_ids])
            * live[:, None, None]
        )
        row_terms = jnp.einsum("kxy,kys->kxs", blocks_now, omega[col_ids], precision=HIGH)
        col_terms = jnp.einsum("kxy,kxs->kys", blocks_now, psi[row_ids], precision=HIGH)
        for member in range(GROUP_SIZE):
            sketch_rows = sketch_rows.at[row_ids[member]].add(row_terms[member])
            sketch_cols = sketch_cols.at[col_ids[member]].add(col_terms[member])
        return (sketch_rows, sketch_cols)

    row_sketch, col_sketch = lax.fori_loop(0, group_count, step, (row_sketch, col_sketch))
    owned_rows = lax.psum_scatter(row_sketch, "col", scatter_dimension=0, tiled=True)
    owned_cols = lax.psum_scatter(col_sketch, "row", scatter_dimension=0, tiled=True)
    finished_rows = apply_factor(gram_of(owned_rows), owned_rows)
    finished_cols = apply_factor(gram_of(owned_cols), owned_cols)
    row_basis = lax.all_to_all(finished_rows, "col", split_axis=1, concat_axis=0, tiled=True)
    col_basis = lax.all_to_all(finished_cols, "row", split_axis=1, concat_axis=0, tiled=True)
    return (row_basis, col_basis)


def solution(mesh):
    placed = (
        P(None, "col"),
        P("col"),
        P("col", None),
        P("col", None, None),
        P("row", None, None),
        P("row", "col", None, None),
    )
    return jax.shard_map(
        per_device,
        mesh=mesh,
        in_specs=placed,
        out_specs=(P("row", "col", None), P("col", "row", None)),
        check_vma=False,
    )
```

profile of v0, /device:TPU:27, one launch (start us, length us, event | category | flops | bytes accessed | tf_op | source)
XLA Modules:
  0.0 737.3 jit_solution(6052222776146654580)
XLA Ops:
  7.2 1.5 fusion.24
  8.7 0.8 convert_reduce_fusion
  16.1 24.5 %all_gather.6 = f32[3,8192]{1,0:T(4,128)S(1)} all-gather(f32[3,1024]{1,0:T(4,128)} %param.20), channel_id=1, replica_groups=mesh['row'=4,'col'=8] {'col'}, dimensions={1}, use_global_device_ids=true | all-gather | bytes 110592 | tf_op jit(solution)/shard_map/all_gather | solution.py:65
  40.6 24.4 %all_gather.7 = f32[8192]{0:T(1024)S(1)} all-gather(f32[1024]{0:T(1024)} %param.21), channel_id=1, replica_groups=mesh['row'=4,'col'=8] {'col'}, dimensions={0}, use_global_device_ids=true | all-gather | bytes 36864 | tf_op jit(solution)/shard_map/all_gather | solution.py:66
  66.1 1.3 gather_fusion.1
  67.4 1.2 gather_fusion.3
  69.8 3.2 mul.274
  73.0 6.9 mul.275
  79.9 3.1 mul.278
  83.0 6.9 mul.279
  89.9 3.1 mul.267
  93.0 6.9 mul.268
  99.9 3.2 mul.288
  103.1 6.9 mul.289
  111.0 6.4 gather_fusion.5
  117.3 4.6 gather_fusion.4
  121.9 8.0 %multiply_multiply_fusion = f32[2,768,768]{2,1,0:T(8,128)S(1)} fusion(f32[2,768,768]{2,1,0:T(8,128)} %mul.289, f32[2,768,768]{2,1,0:T(8,128)} %mul.279, f32[2,768,768]{2,1,0:T(8,128)} %mul.275, f32[2,768,768]{2,1,0:T(8,128)} %mul.268, f32[2]{0:T(128)S(1)} %convert_reduce_fusion, f32[768]{0:T(1024)S(1)} %broadcast_bitcast_fusion, f32[768,768]{1,0:T(8,128)S(1)} %bitcast.126), kind=kLoop, calls=%fused_computation.22 | loop fusion | flops 9437184 | bytes 25955336 | tf_op jit(solution)/shard_map/while/body/mul | solution.py:105
  129.9 7.8 %fusion.33 = f32[2,768,256]{2,1,0:T(8,128)S(1)} fusion(f32[2,768,768]{2,1,0:T(8,128)S(1)} %multiply_multiply_fusion, f32[2,768,256]{2,1,0:T(8,128)S(1)} %copy-done.3), kind=kOutput, calls=%fused_computation.120 | convolution fusion | flops 3623878656 | bytes 7864320 | tf_op jit(solution)/shard_map/while/body/kxy,kxs->kys/dot_general | solution.py:109
  137.7 4.2 fusion.32
  144.4 1.2 broadcast_in_dim.9
  145.6 7.7 %multiply_select_fusion = (f32[8,768,256]{2,1,0:T(8,128)}, f32[16,768,256]{2,1,0:T(8,128)S(1)}) fusion(f32[16,768,256]{2,1,0:T(8,128)} %param.24, s32[]{:T(128)S(6)} %min.4, f32[8,768]{1,0:T(8,128)S(1)} %copy-done.8, pred[]{:T(512)S(6)} %eq.12, f32[16,768,256]{2,1,0:T(8,128)S(1)} %broadcast_in_dim.9, f32[8,768,256]{2,1,0:T(8,128)} %param.23), kind=kLoop, calls=%fused_computation.20 | loop fusion | flops 6291456 | bytes 25190404 | tf_op jit(solution)/shard_map/jit(_where)/select_n | solution.py:87
  153.3 1.0 and_reduce_fusion
  154.3 3.6 copy-done
  157.9 18.2 %while.22 = (s32[]{:T(128)}, f32[16,768,256]{2,1,0:T(8,128)}, f32[8,768,256]{2,1,0:T(8,128)}, s32[]{:T(128)}, pred[]{:T(512)}, /*index=5*/s32[2,2]{1,0:T(2,128)S...) while((s32[]{:T(128)}, f32[16,768,256]{2,1,0:T(8,128)}, ...), condition=%wide.region_7.8_spmd, body=%wide.region_6.7_spmd.sunk | while | flops 1572882 | bytes 9439589 | solution.py:115
  162.9 3.9 fusion.61
  168.7 2.7 fusion.62
  173.3 2.8 fusion.63
  177.0 71.6 %reduce-scatter.5.cloned.1.call-done = f32[2,768,256]{2,1,0:T(8,128)} async-done(((f32[8,768,256]{2,1,0:T(8,128)}), f32[2,768,256]{2,1,0:T(8,128)}) %reduce-scatter.5.cloned.1.call-update) | async-done | bytes 1572880 | tf_op jit(solution)/shard_map/reduce_scatter | solution.py:117
  248.6 4.6 fusion.35
  253.5 0.8 copy-done.5
  254.3 23.5 %custom-call.21 = f32[2,128,128]{2,1,0:T(8,128)S(1)} custom-call(f32[2,128,128]{2,1,0:T(8,128)S(1)} %cholesky.201), custom_call_target="Cholesky" | custom-call | tf_op jit(solution)/shard_map/jit(cholesky)/cholesky | solution.py:52
  277.8 180.4 %reduce-scatter.3.cloned.1.call-done = f32[2,768,256]{2,1,0:T(8,128)} async-done(((f32[16,768,256]{2,1,0:T(8,128)}), f32[2,768,256]{2,1,0:T(8,128)}) %reduce-scatter.3.cloned.1.call-update) | async-done | bytes 1572880 | tf_op jit(solution)/shard_map/reduce_scatter | solution.py:116
  458.2 4.7 fusion.34
  463.9 23.5 %custom-call.17 = f32[2,128,128]{2,1,0:T(8,128)S(1)} custom-call(f32[2,128,128]{2,1,0:T(8,128)S(1)} %cholesky.198), custom_call_target="Cholesky" | custom-call | tf_op jit(solution)/shard_map/jit(cholesky)/cholesky | solution.py:52
  487.5 19.9 %custom-call.18 = f32[2,1,128,128]{2,3,1,0:T(8,128)S(1)} custom-call(f32[2,1,128,128]{3,2,1,0:T(8,128)S(1)} %get-tuple-element.296), custom_call_target="InvertDiagBlocksLowerTriangular" | custom-call | tf_op jit(solution)/shard_map/jit(cholesky)/cholesky | solution.py:52
  507.4 1.2 constant_dynamic-update-slice_fusion.3
  508.5 1.3 convolution_subtract_fusion.3
  509.9 23.5 %custom-call.19 = f32[2,128,128]{2,1,0:T(8,128)S(1)} custom-call(f32[2,128,128]{2,1,0:T(8,128)S(1)} %convolution_subtract_fusion.3), custom_call_target="Cholesky" | custom-call | tf_op jit(solution)/shard_map/jit(cholesky)/cholesky | solution.py:52
  533.3 19.7 %custom-call.22 = f32[2,1,128,128]{2,3,1,0:T(8,128)S(1)} custom-call(f32[2,1,128,128]{3,2,1,0:T(8,128)S(1)} %get-tuple-element.295), custom_call_target="InvertDiagBlocksLowerTriangular" | custom-call | tf_op jit(solution)/shard_map/jit(cholesky)/cholesky | solution.py:52
  553.0 1.2 constant_dynamic-update-slice_fusion.1
  554.2 1.3 convolution_subtract_fusion.2
  555.5 23.9 %custom-call.23 = f32[2,128,128]{2,1,0:T(8,128)S(1)} custom-call(f32[2,128,128]{2,1,0:T(8,128)S(1)} %convolution_subtract_fusion.2), custom_call_target="Cholesky" | custom-call | tf_op jit(solution)/shard_map/jit(cholesky)/cholesky | solution.py:52
  579.9 1.0 select_select_fusion
  581.0 4.0 while.24
  581.6 1.4 bitcast_dynamic-update-slice_fusion.5
  583.6 1.4 bitcast_dynamic-update-slice_fusion.5
  585.0 39.3 %custom-call.24 = f32[2,2,128,128]{2,3,1,0:T(8,128)S(1)} custom-call(f32[2,2,128,128]{3,2,1,0:T(8,128)S(1)} %bitcast.135), custom_call_target="InvertDiagBlocksLowerTriangular" | custom-call | tf_op jit(solution)/shard_map/triangular_solve/custom-call.0 | solution.py:53
  624.4 0.9 fusion.4
  625.2 1.4 convolution_subtract_fusion
  626.6 0.9 fusion.13
  627.6 2.1 copy.114
  629.7 4.1 all-to-all-start.1
  633.8 6.0 while.23
  634.5 2.3 bitcast_dynamic-update-slice_fusion.4
  637.5 2.3 bitcast_dynamic-update-slice_fusion.4
  639.8 39.9 %custom-call.20 = f32[2,2,128,128]{2,3,1,0:T(8,128)} custom-call(f32[2,2,128,128]{3,2,1,0:T(8,128)S(1)} %bitcast.134), custom_call_target="InvertDiagBlocksLowerTriangular" | custom-call | tf_op jit(solution)/shard_map/triangular_solve/custom-call.0 | solution.py:53
  679.8 1.8 fusion.6
  681.5 2.3 convolution_subtract_fusion.1
  683.8 1.8 fusion.17
  685.7 2.1 copy.103
  687.8 5.7 all-to-all-start
  693.6 1.3 copy.116
  694.9 33.9 %all-to-all-done = f32[2,768,256]{2,0,1:T(2,128)S(1)} async-done(((f32[2,768,256]{2,0,1:T(2,128)}), f32[2,768,256]{2,0,1:T(2,128)S(1)}, u32[]{:S(2)}, u32[]{:S(2)}) %all-to-all-start) | async-done | bytes 1572896 | tf_op jit(solution)/shard_map/all_to_all | solution.py:120
  729.0 1.3 copy.105
  (87 shorter events, 11.3 us)
Async XLA Ops:
  7.2 241.4 %reduce-scatter.5.cloned.1.call-start = ((), (), s32[]{:S(2)}) async-start(), calls=%async_computation.5 | async-start | bytes 7864320 | tf_op jit(solution)/shard_map/reduce_scatter | solution.py:117
  110.0 0.8 copy-start.9
  121.9 8.0 %copy-start.3 = (f32[2,768,256]{2,1,0:T(8,128)S(1)}, f32[2,768,256]{2,1,0:T(8,128)}, u32[]{:S(2)}) copy-start(f32[2,768,256]{2,1,0:T(8,128)} %gather_fusion.5) | copy-start | bytes 4718596
  129.9 7.8 %copy-start.4 = (f32[2,768,256]{2,1,0:T(8,128)S(1)}, f32[2,768,256]{2,1,0:T(8,128)}, u32[]{:S(2)}) copy-start(f32[2,768,256]{2,1,0:T(8,128)} %gather_fusion.4) | copy-start | bytes 4718596
  144.4 1.2 copy-start.8
  145.6 7.7 %copy-start.10 = (s32[3]{0:T(128)S(1)}, s32[3]{0:T(128)}, u32[]{:S(2)}) copy-start(s32[3]{0:T(128)} %constant.253.clone.1) | copy-start | bytes 40
  145.6 7.7 %copy-start.11 = (s32[3]{0:T(128)S(1)}, s32[3]{0:T(128)}, u32[]{:S(2)}) copy-start(s32[3]{0:T(128)} %constant.255.clone.1) | copy-start | bytes 40
  145.6 12.3 %copy-start.7 = (s32[1,1,2,2]{3,2,1,0:T(2,128)S(1)}, s32[1,1,2,2]{3,2,1,0:T(2,128)}, u32[]{:S(2)}) copy-start(s32[1,1,2,2]{3,2,1,0:T(2,128)} %param.25) | copy-start | bytes 52
  153.3 4.6 copy-start
  176.1 282.0 %reduce-scatter.3.cloned.1.call-start = ((), (), s32[]{:S(2)}) async-start(), calls=%async_computation.4 | async-start | bytes 14155776 | tf_op jit(solution)/shard_map/reduce_scatter | solution.py:116
  253.5 0.8 copy-start.5
  463.0 161.3 %copy-start.2 = (f32[2,768,256]{2,1,0:T(8,128)S(1)}, f32[2,768,256]{2,1,0:T(8,128)}, u32[]{:S(2)}) copy-start(f32[2,768,256]{2,1,0:T(8,128)} %reduce-scatter.5.cloned.1.call-done) | copy-start | bytes 4718596
  463.1 0.8 copy-start.6
  627.6 52.1 %copy-start.1 = (f32[2,768,256]{2,1,0:T(8,128)S(1)}, f32[2,768,256]{2,1,0:T(8,128)}, u32[]{:S(2)}) copy-start(f32[2,768,256]{2,1,0:T(8,128)} %reduce-scatter.3.cloned.1.call-done) | copy-start | bytes 4718596
  629.7 58.1 %all-to-all-start.1 = ((f32[2,768,256]{2,0,1:T(2,128)}), f32[2,768,256]{2,0,1:T(2,128)S(1)}, u32[]{:S(2)}, u32[]{:S(2)}) async-start(f32[2,768,256]{2,0,1:T(2,128)} %copy.114), calls=%async_computation.3 | async-start | bytes 3145728 | tf_op jit(solution)/shard_map/all_to_all | solution.py:121
  687.8 41.0 %all-to-all-start = ((f32[2,768,256]{2,0,1:T(2,128)}), f32[2,768,256]{2,0,1:T(2,128)S(1)}, u32[]{:S(2)}, u32[]{:S(2)}) async-start(f32[2,768,256]{2,0,1:T(2,128)} %copy.103), calls=%async_computation.1 | async-start | bytes 3145728 | tf_op jit(solution)/shard_map/all_to_all | solution.py:120
Sparse Core Ops, SparseCore 0:
  176.3 72.2 reduce-scatter.4
  252.1 205.9 reduce-scatter.2
where the time goes:
time: 747 us; the launch traced here: 737 us
  waiting for transfers between devices  287 us (38%)
  other arithmetic  244 us (33%)
  local copies, waits for them, and re-layouts  82.3 us (11%)
  blocking collectives  48.8 us (7%)
  matrix products  35.2 us (5%)
  between operations  22.8 us (3%)
  starting transfers between devices  9.83 us (1%)
  loops' own time  7.78 us (1%)
    reduce_scatter x1, waiting for transfers between devices, per_device(): lax.psum_scatter(row_sketch, 'col', scatter_dimension=0, tiled=True)  180 us
    another operation x16, other arithmetic, apply_factor(): factor = jnp.linalg.cholesky(gram)  134 us
    another operation x7, other arithmetic, apply_factor(): lax.linalg.triangular_solve(factor, sketch, left_side=False, lower=True,...  80.5 us
    reduce_scatter x1, waiting for transfers between devices, per_device(): lax.psum_scatter(col_sketch, 'row', scatter_dimension=0, tiled=True)  71.6 us
    all_to_all x1, waiting for transfers between devices, per_device(): lax.all_to_all(finished_rows, 'col', split_axis=1, concat_axis=0, tiled=T...  33.9 us
    all_gather x1, blocking collectives, per_device(): lax.all_gather(positions, 'col', axis=1, tiled=True)  24.5 us
    all_gather x1, blocking collectives, per_device(): lax.all_gather(modulus, 'col', axis=0, tiled=True)  24.4 us
  transfers between devices with their start and end apart: 4, of which 3 were waited for; matrix products, arithmetic and copies ran while one was open for 11% of the time, Pallas kernels for 0%

commit v1 on v0

v1 whole, which is shorter than its diff:
```python
import functools

import jax
import jax.numpy as jnp
from jax import lax
from jax.experimental import pallas as pl
from jax.experimental.pallas import tpu as pltpu
from jax.sharding import PartitionSpec as P

COUPLE = 0.25
ROOT_TWO = 1.4142135623730951
HIGH = lax.Precision.HIGHEST
BASE = 64
LANES = 128
MESH = pl.DeviceIdType.MESH
ANY = pl.BlockSpec(memory_space=pl.ANY)


def exchange(outgoing, incoming, barrier, send_sem, recv_sem, local_sem):
    row = lax.axis_index("row")
    col = lax.axis_index("col")
    remote_out = jnp.int32(0)
    for _, device, _, cond in incoming:
        here = jnp.logical_and(device[0] == row, device[1] == col)

        @pl.when(jnp.logical_and(cond, jnp.logical_not(here)))
        def _():
            pl.semaphore_signal(barrier, inc=1, device_id=device, device_id_type=MESH)

    for _, _, device, _, cond in outgoing:
        here = jnp.logical_and(device[0] == row, device[1] == col)
        remote_out = remote_out + jnp.logical_and(cond, jnp.logical_not(here)).astype(jnp.int32)
    pl.semaphore_wait(barrier, remote_out)

    def each_out(action):
        for number, (src, dst, device, slot, cond) in enumerate(outgoing):
            here = jnp.logical_and(device[0] == row, device[1] == col)
            remote = pltpu.make_async_remote_copy(
                src_ref=src,
                dst_ref=dst,
                send_sem=send_sem.at[number],
                recv_sem=recv_sem.at[slot],
                device_id=device,
                device_id_type=MESH,
            )
            local = pltpu.make_async_copy(src, dst, local_sem.at[number])

            @pl.when(jnp.logical_and(cond, jnp.logical_not(here)))
            def _():
                remote.start() if action == "start" else remote.wait_send()

            @pl.when(jnp.logical_and(cond, here))
            def _():
                local.start() if action == "start" else local.wait()

    each_out("start")
    for dst, device, slot, cond in incoming:
        here = jnp.logical_and(device[0] == row, device[1] == col)

        @pl.when(jnp.logical_and(cond, jnp.logical_not(here)))
        def _():
            pltpu.make_async_remote_copy(
                src_ref=dst,
                dst_ref=dst,
                send_sem=send_sem.at[0],
                recv_sem=recv_sem.at[slot],
                device_id=device,
                device_id_type=MESH,
            ).wait_recv()

    each_out("wait")


def remote_call(body, out_shapes, sems_out, sems_in, ident, operands):
    return pl.pallas_call(
        body,
        out_shape=out_shapes,
        in_specs=[ANY] * len(operands),
        out_specs=[ANY] * len(out_shapes),
        scratch_shapes=[
            pltpu.SemaphoreType.DMA((sems_out,)),
            pltpu.SemaphoreType.DMA((sems_in,)),
            pltpu.SemaphoreType.DMA((sems_out,)),
        ],
        compiler_params=pltpu.CompilerParams(collective_id=ident, has_side_effects=True),
        name="exchange_%d" % ident,
    )(*operands)


def f32(*shape):
    return jax.ShapeDtypeStruct(shape, jnp.float32)


def gather_kernel(sizes, points_ref, meta_ref, out_points, out_meta, send_sem, recv_sem, local_sem):
    n_row, n_col, ratio = sizes
    row = lax.axis_index("row")
    col = lax.axis_index("col")
    yes = jnp.bool_(True)
    outgoing, incoming = [], []
    owner_here = col // ratio == row
    for c in range(n_col):
        outgoing.append((points_ref, out_points.at[lax.rem(col, ratio)], (row, c), lax.rem(col, ratio), owner_here))
    for x in range(ratio):
        incoming.append((out_points.at[x], (row, row * ratio + x), x, yes))
    for q in range(n_col):
        outgoing.append(
            (meta_ref, out_meta.at[col], (q // ratio, row * ratio + q % ratio), ratio + col, yes)
        )
        incoming.append((out_meta.at[q], (col // ratio, q), ratio + q, yes))
    for p in range(n_row):
        outgoing.append((meta_ref, out_meta.at[n_col + row], (p, col), ratio + n_col + row, yes))
        incoming.append((out_meta.at[n_col + p], (p, col), ratio + n_col + p, yes))
    exchange(outgoing, incoming, pltpu.get_barrier_semaphore(), send_sem, recv_sem, local_sem)


def spread_kernel(
    sizes, row_terms, col_terms, psi, out_rows, out_cols, out_psi, send_sem, recv_sem, local_sem
):
    n_row, n_col, ratio, own = sizes
    row = lax.axis_index("row")
    col = lax.axis_index("col")
    yes = jnp.bool_(True)
    row_part = row_terms.shape[1] // n_col
    col_part = col_terms.shape[1] // n_row
    outgoing, incoming = [], []
    for q in range(n_col):
        outgoing.append(
            (
                row_terms.at[:, q * row_part : (q + 1) * row_part],
                out_rows.at[col],
                (q // ratio, row * ratio + q % ratio),
                col,
                yes,
            )
        )
        incoming.append((out_rows.at[q], (col // ratio, q), q, yes))
    for p in range(n_row):
        outgoing.append(
            (col_terms.at[:, p * col_part : (p + 1) * col_part], out_cols.at[row], (p, col), n_col + row, yes)
        )
        incoming.append((out_cols.at[p], (p, col), n_col + p, yes))
    has_psi = col // ratio == row
    first = lax.rem(col, ratio) * (own * n_row)
    for p in range(n_row):
        outgoing.append((psi.at[pl.ds(first + p * own, own)], out_psi, (p, col), n_col + n_row, has_psi))
    incoming.append((out_psi, (col // ratio, col), n_col + n_row, yes))
    exchange(outgoing, incoming, pltpu.get_barrier_semaphore(), send_sem, recv_sem, local_sem)


def collect_kernel(sizes, rows, cols, out_rows, out_cols, send_sem, recv_sem, local_sem):
    n_row, n_col, ratio, own = sizes
    row = lax.axis_index("row")
    col = lax.axis_index("col")
    yes = jnp.bool_(True)
    group = col // ratio
    mine = row * ratio + lax.rem(col, ratio)
    outgoing, incoming = [], []
    for q in range(n_col):
        device = (q // ratio, group * ratio + q % ratio)
        start = (q % ratio) * (own * n_row) + (q // ratio) * own
        outgoing.append((rows.at[pl.ds(start, own)], out_rows.at[mine], device, mine, yes))
        incoming.append((out_rows.at[q], device, q, yes))
    for p in range(n_row):
        outgoing.append((cols.at[pl.ds(p * own, own)], out_cols.at[row], (p, col), n_col + row, yes))
        incoming.append((out_cols.at[p], (p, col), n_col + p, yes))
    exchange(outgoing, incoming, pltpu.get_barrier_semaphore(), send_sem, recv_sem, local_sem)


def deliver_kernel(sizes, rows, cols, out_rows, out_cols, send_sem, recv_sem, local_sem):
    n_row, n_col, ratio, own = sizes
    row = lax.axis_index("row")
    col = lax.axis_index("col")
    yes = jnp.bool_(True)
    row_part = rows.shape[1] // n_col
    col_part = cols.shape[1] // n_row
    outgoing, incoming = [], []
    mine = row * ratio + lax.rem(col, ratio)
    place = lax.rem(col, ratio) * (own * n_row) + row * own
    for c in range(n_col):
        outgoing.append(
            (
                rows.at[:, c * row_part : (c + 1) * row_part],
                out_rows.at[pl.ds(place, own)],
                (col // ratio, c),
                mine,
                yes,
            )
        )
        start = (c % ratio) * (own * n_row) + (c // ratio) * own
        incoming.append((out_rows.at[pl.ds(start, own)], (c // ratio, row * ratio + c % ratio), c, yes))
    for p in range(n_row):
        outgoing.append(
            (
                cols.at[:, p * col_part : (p + 1) * col_part],
                out_cols.at[pl.ds(row * own, own)],
                (p, col),
                n_col + row,
                yes,
            )
        )
        incoming.append((out_cols.at[pl.ds(p * own, own)], (p, col), n_col + p, yes))
    exchange(outgoing, incoming, pltpu.get_barrier_semaphore(), send_sem, recv_sem, local_sem)


def dot(a, b, contract):
    return lax.dot_general(
        a, b, (contract, ((), ())), precision=HIGH, preferred_element_type=jnp.float32
    )


def terms_kernel(pairs, left_ref, right_ref, omega_ref, psi_ref, row_ref, col_ref):
    slot = pl.program_id(0)
    live = pairs[slot, 0] >= 0
    zones = right_ref.shape[2]

    @pl.when(jnp.logical_not(live))
    def _():
        row_ref[...] = jnp.zeros_like(row_ref)
        col_ref[...] = jnp.zeros_like(col_ref)

    @pl.when(live)
    def _():
        offs = [left_ref[0, :, n : n + 1] - right_ref[0, n : n + 1, :] for n in range(3)]
        spread = (offs[0] * offs[0] + offs[1] * offs[1] + offs[2] * offs[2]) + 1.0
        inverse = lax.rsqrt(spread)
        nx, ny, nz = [o * inverse for o in offs]
        weight = COUPLE * inverse * inverse * inverse * left_ref[0, :, 3:4] * right_ref[0, 3:4, :]
        u = [nx * nx, ny * ny, nz * nz, ROOT_TWO * ny * nz, ROOT_TWO * nx * nz, ROOT_TWO * nx * ny]
        for p in range(6):
            parts = []
            for q in range(6):
                val = -5.0 * u[p] * u[q]
                if q < 3:
                    val = val + u[p]
                if p < 3:
                    val = val + u[q]
                if p == q:
                    val = val + 1.0
                parts.append(weight * val)
            strip = jnp.concatenate(parts, axis=1)
            span = slice(p * zones, (p + 1) * zones)
            row_ref[0, span, :] = dot(strip, omega_ref[0], ((1,), (0,)))
            term = dot(strip, psi_ref[0, span, :], ((0,), (0,)))
            if p == 0:
                col_ref[0] = term
            else:
                col_ref[0] += term


def add_kernel(ids, terms_ref, out_ref):
    count = terms_ref.shape[0]
    slots = terms_ref.shape[1]
    out_ref[...] = jnp.zeros_like(out_ref)

    @pl.loop(0, count * slots)
    def _(n):
        target = ids[n]

        @pl.when(target >= 0)
        def _():
            out_ref[target] += terms_ref[n // slots, n % slots]


def sum_terms(terms, ids, clusters):
    part = terms.shape[2]
    width = terms.shape[3]
    return pl.pallas_call(
        add_kernel,
        out_shape=f32(clusters, part, width),
        grid_spec=pltpu.PrefetchScalarGridSpec(
            num_scalar_prefetch=1,
            grid=(1,),
            in_specs=[pl.BlockSpec(terms.shape, lambda n, _: (0, 0, 0, 0), pipeline_mode=pl.Buffered(1))],
            out_specs=pl.BlockSpec((clusters, part, width), lambda n, _: (0, 0, 0), pipeline_mode=pl.Buffered(1)),
        ),
        name="sum_terms",
    )(ids, terms)


def invert_base(blocks):
    size = blocks[0].shape[0]
    rows = lax.broadcasted_iota(jnp.int32, (size, size), 0)
    cols = lax.broadcasted_iota(jnp.int32, (size, size), 1)
    eye = (rows == cols).astype(jnp.float32)
    work = [jnp.concatenate([b, eye], axis=1) for b in blocks]
    done = [[] for _ in blocks]
    for k in range(size):
        low = (k // 8) * 8
        nxt = []
        for m, w in enumerate(work):
            at = k - low
            pivot_row = w[at : at + 1, :]
            d = pivot_row[:, k : k + 1]
            root = lax.rsqrt(d)
            scaled = pivot_row * root
            done[m].append(scaled[:, size:])
            if k + 1 < size:
                column = w[:, k : k + 1] * root
                if at == 7:
                    nxt.append(w[8:] - column[8:] * scaled)
                else:
                    nxt.append(w - column * scaled)
        work = nxt
    return [jnp.concatenate(d, axis=0) for d in done]


def basis_kernel(own, row_terms, col_terms, omega_ref, psi_ref, weight_ref, row_ref, col_ref, aug):
    width = omega_ref.shape[2]
    for k in range(own):
        for terms, start, out in ((row_terms, omega_ref, row_ref), (col_terms, psi_ref, col_ref)):
            pieces = terms.shape[0]
            part = terms.shape[2]
            for c in range(pieces):
                span = slice(c * part, (c + 1) * part)
                out[k, span, :] = weight_ref[k, span, :] * start[k, span, :] + terms[c, k]
    rows = lax.broadcasted_iota(jnp.int32, (width, width), 0)
    cols = lax.broadcasted_iota(jnp.int32, (width, width), 1)
    eye = (rows == cols).astype(jnp.float32)
    sources = [(out, k) for k in range(own) for out in (row_ref, col_ref)]
    for m, (out, k) in enumerate(sources):
        aug[m, :, :width] = dot(out[k], out[k], ((0,), (0,)))
        aug[m, :, width:] = eye
    steps = width // BASE
    lane = lax.broadcasted_iota(jnp.int32, (BASE, width), 1)
    for s in range(steps):
        span = slice(s * BASE, (s + 1) * BASE)
        inverses = invert_base([aug[m, span, span] for m in range(len(sources))])
        for m in range(len(sources)):
            panel = dot(inverses[m], aug[m, span, :], ((1,), (0,)))
            aug[m, span, :] = panel
            if s + 1 < steps:
                rest = slice((s + 1) * BASE, width)
                update = dot(jnp.where(lane >= (s + 1) * BASE, panel[:, :width], 0.0), panel, ((0,), (0,)))
                aug[m, rest, :] = aug[m, rest, :] - update[(s + 1) * BASE :]
    for m, (out, k) in enumerate(sources):
        out[k] = dot(out[k], aug[m, :, width:], ((1,), (1,)))


def per_device(positions, modulus, self_weight, omega, psi, blocks, *, n_row, n_col):
    col_clusters, height, width = omega.shape
    row_clusters = psi.shape[0]
    zones = positions.shape[1] // col_clusters
    ratio = row_clusters // col_clusters
    own = col_clusters // n_row
    row = lax.axis_index("row")
    col = lax.axis_index("col")
    pairs = blocks.reshape(-1, 2)
    slots = pairs.shape[0]

    points = jnp.concatenate([positions, modulus[None]], axis=0)
    meta = jnp.pad(pairs.astype(jnp.float32).reshape(1, -1), ((0, 7), (0, LANES - 2 * slots)))
    all_points, all_meta = remote_call(
        functools.partial(gather_kernel, (n_row, n_col, ratio)),
        [f32(ratio, 4, positions.shape[1]), f32(n_col + n_row, 8, LANES)],
        2 * n_col + n_row,
        ratio + n_col + n_row,
        1,
        [points, meta],
    )
    row_points = all_points.reshape(ratio, 4, col_clusters, zones).transpose(0, 2, 3, 1)
    row_points = row_points.reshape(row_clusters, zones, 4)
    col_points = points.reshape(4, col_clusters, zones).transpose(1, 0, 2)
    metas = all_meta[:, 0, : 2 * slots].astype(jnp.int32).reshape(n_col + n_row, slots, 2)
    row_ids = metas[:n_col, :, 0].reshape(-1)
    col_ids = metas[n_col:, :, 1].reshape(-1)

    row_terms, col_terms = pl.pallas_call(
        terms_kernel,
        out_shape=[f32(slots, height, width), f32(slots, height, width)],
        grid_spec=pltpu.PrefetchScalarGridSpec(
            num_scalar_prefetch=1,
            grid=(slots,),
            in_specs=[
                pl.BlockSpec((1, zones, 4), lambda n, ids: (jnp.maximum(ids[n, 0], 0), 0, 0)),
                pl.BlockSpec((1, 4, zones), lambda n, ids: (jnp.maximum(ids[n, 1], 0), 0, 0)),
                pl.BlockSpec((1, height, width), lambda n, ids: (jnp.maximum(ids[n, 1], 0), 0, 0)),
                pl.BlockSpec((1, height, width), lambda n, ids: (jnp.maximum(ids[n, 0], 0), 0, 0)),
            ],
            out_specs=[
                pl.BlockSpec((1, height, width), lambda n, ids: (n, 0, 0)),
                pl.BlockSpec((1, height, width), lambda n, ids: (n, 0, 0)),
            ],
        ),
        name="terms",
    )(pairs, row_points, col_points, omega, psi)

    sizes = (n_row, n_col, ratio, own)
    row_part = height // n_col
    col_part = height // n_row
    got_rows, got_cols, own_psi = remote_call(
        functools.partial(spread_kernel, sizes),
        [
            f32(n_col, slots, row_part, width),
            f32(n_row, slots, col_part, width),
            f32(own, height, width),
        ],
        n_col + 2 * n_row,
        n_col + n_row + 1,
        2,
        [row_terms, col_terms, psi],
    )
    row_chunks = sum_terms(got_rows, row_ids, row_clusters)
    col_chunks = sum_terms(got_cols, col_ids, col_clusters)
    full_rows, full_cols = remote_call(
        functools.partial(collect_kernel, sizes),
        [f32(n_col, own, row_part, width), f32(n_row, own, col_part, width)],
        n_col + n_row,
        n_col + n_row,
        3,
        [row_chunks, col_chunks],
    )
    own_omega = lax.dynamic_slice_in_dim(omega, row * own, own, 0)
    own_weight = lax.dynamic_slice_in_dim(self_weight, row * own, own, 0)[:, :, None]
    full = pl.BlockSpec(memory_space=pltpu.VMEM)
    row_basis, col_basis = pl.pallas_call(
        functools.partial(basis_kernel, own),
        out_shape=[f32(own, height, width), f32(own, height, width)],
        in_specs=[full] * 5,
        out_specs=[full] * 2,
        scratch_shapes=[pltpu.VMEM((2 * own, width, 2 * width), jnp.float32)],
        name="basis",
    )(full_rows, full_cols, own_omega, own_psi, own_weight)
    return tuple(
        remote_call(
            functools.partial(deliver_kernel, sizes),
            [f32(row_clusters, row_part, width), f32(col_clusters, col_part, width)],
            n_col + n_row,
            n_col + n_row,
            4,
            [row_basis, col_basis],
        )
    )


def solution(mesh):
    placed = (
        P(None, "col"),
        P("col"),
        P("col", None),
        P("col", None, None),
        P("row", None, None),
        P("row", "col", None, None),
    )
    return jax.shard_map(
        functools.partial(per_device, n_row=mesh.shape["row"], n_col=mesh.shape["col"]),
        mesh=mesh,
        in_specs=placed,
        out_specs=(P("row", "col", None), P("col", "row", None)),
        check_vma=False,
    )
```

time: 747 us -> 262 us (0.35); the launches traced: 737 us -> 260 us
  waiting for transfers between devices: 287 us -> 0 us
  Pallas kernels: 0 us -> 243 us
  other arithmetic: 244 us -> 4.18 us
  local copies, waits for them, and re-layouts: 82.3 us -> 12.1 us
  blocking collectives: 48.8 us -> 0 us
  matrix products: 35.2 us -> 0 us
  between operations: 22.8 us -> 0.7 us
  starting transfers between devices: 9.83 us -> 0 us
  loops' own time: 7.78 us -> 0 us
    reduce_scatter x2 -> x0, waiting for transfers between devices: 252 us -> none  [the longest x1 180 us: per_device(): lax.psum_scatter(row_sketch, 'col', scatter_dimension=0, tiled=True)]
    pallas_call x0 -> x8, Pallas kernels: none -> 243 us  [the longest x4 185 us: remote_call(): pl.pallas_call(body, out_shape=out_shapes, in_specs=[ANY] * len(operands)...]
    another operation x25 -> x0, other arithmetic: 216 us -> none  [the longest x16 134 us: apply_factor(): factor = jnp.linalg.cholesky(gram)]
    all_gather x2 -> x0, blocking collectives: 48.8 us -> none  [the longest x1 24.5 us: per_device(): lax.all_gather(positions, 'col', axis=1, tiled=True)]
    mul x9 -> x0, local copies, waits for them, and re-layouts: 40.3 us -> none  [the longest x2 10.1 us: make_tiles(): trace_vec[None, :, None, None, None] * voigt_col]
    all_to_all x2 -> x0, waiting for transfers between devices: 33.9 us -> none  [the longest x1 33.9 us: per_device(): lax.all_to_all(finished_rows, 'col', split_axis=1, concat_axis=0, tiled=T...]
    dot_general x4 -> x0, matrix products: 21.2 us -> none  [the longest x2 9.3 us: gram_of(): return jnp.einsum('kxs,kxt->kst', sketch, sketch, precision=HIGH)]
    gather x6 -> x0, local copies, waits for them, and re-layouts: 14.6 us -> none  [the longest x1 6.36 us: step(): psi[row_ids]]
  transfers between devices with their start and end apart: 4 -> 0, of which waited for: 3 -> 0; matrix products, arithmetic and copies ran while one was open for 11% -> 0% of each run, Pallas kernels for 0% -> 0%
where the time goes in v1:
time: 262 us; the launch traced here: 260 us
  Pallas kernels  243 us (93%)
  local copies, waits for them, and re-layouts  12.1 us (5%)
  other arithmetic  4.18 us (2%)
    pallas_call x4, Pallas kernels, remote_call(): pl.pallas_call(body, out_shape=out_shapes, in_specs=[ANY] * len(operands)...  185 us
    pallas_call x1, Pallas kernels, per_device(): pl.pallas_call(functools.partial(basis_kernel, own), out_shape=[f32(own,...  41.1 us
    pallas_call x1, Pallas kernels, per_device(): pl.pallas_call(terms_kernel, out_shape=[f32(slots, height, width), f32(sl...  9.97 us
    pallas_call x2, Pallas kernels, sum_terms(): pl.pallas_call(add_kernel, out_shape=f32(clusters, part, width), grid_spe...  7.15 us

profile of v1, /device:TPU:27, one launch (start us, length us, event | category | flops | bytes accessed | tf_op | source)
XLA Modules:
  0.0 259.8 jit_solution(8854812612684950521)
XLA Ops:
  0.6 0.0 copy-start
  0.6 1.4 pad_maximum_fusion.points_ref
  2.0 0.7 convert_element_type.22
  2.7 0.1 convert_element_type.23
  2.8 0.6 pad.4.meta_ref
  3.4 7.9 %exchange_1.1 = (f32[2,4,1024]{2,1,0:T(4,128)}, f32[12,8,128]{2,1,0:T(8,128)}) custom-call(f32[4,1024]{1,0:T(4,128)} %pad_maximum_fusion.points_ref, f32[8,128]{1,0:T(8,128)} %pad.4.meta_ref), custom_call_target="tpu_custom_call" | custom-call | tf_op jit(solution)/shard_map/exchange_1/pallas_call | solution.py:75
  11.3 2.1 copy.22
  13.4 1.3 maximum_bitcast_fusion.right_ref
  14.7 10.0 %terms.1 = (f32[2,768,256]{2,1,0:T(8,128)}, f32[2,768,256]{2,1,0:T(8,128)}) custom-call(s32[2,2]{1,0:T(2,128)} %bitcast.24, f32[16,128,4]{2,1,0:T(8,128)} %bitcast.18, f32[8,4,128]{2,1,0:T(4,128)} %maximum_bitcast_fusion.right_ref, f32[8,768,256]{2,1,0:T(8,128)} %omega_ref.1, f32[16,768,256]{2,1,0:T(8,128)} %psi.1), custom_call_target="tpu_custom_call" | custom-call | tf_op jit(solution)/shard_map/terms/pallas_call | solution.py:367
  24.7 89.0 %exchange_2.1 = (f32[8,2,96,256]{3,2,1,0:T(8,128)}, f32[4,2,192,256]{3,2,1,0:T(8,128)}, f32[2,768,256]{2,1,0:T(8,128)}) custom-call(f32[2,768,256]{2,1,0:T(8,128)} %get-tuple-element.15.row_terms, f32[2,768,256]{2,1,0:T(8,128)} %get-tuple-element.16.col_terms, f32[16,768,256]{2,1,0:T(8,128)} %psi.1), custom_call_target="tpu_custom_call" | custom-call | tf_op jit(solution)/shard_map/exchange_2/pallas_call | solution.py:75
  113.7 0.8 slice_convert_fusion
  114.5 0.1 copy.17
  114.6 0.1 slice.13
  114.6 0.1 copy.20
  114.7 0.6 reshape_squeeze.7.ids
  115.3 3.5 %sum_terms.3.cols = f32[8,192,256]{2,1,0:T(8,128)} custom-call(s32[8]{0:T(128)} %reshape_squeeze.7.ids, f32[4,2,192,256]{3,2,1,0:T(8,128)} %get-tuple-element.18.terms_ref), custom_call_target="tpu_custom_call" | custom-call | tf_op jit(solution)/shard_map/sum_terms/pallas_call | solution.py:267
  118.9 0.1 copy.18
  118.9 0.6 reshape_squeeze.6.ids
  119.5 3.6 %sum_terms.2.rows = f32[16,96,256]{2,1,0:T(8,128)} custom-call(s32[16]{0:T(128)} %reshape_squeeze.6.ids, f32[8,2,96,256]{3,2,1,0:T(8,128)} %get-tuple-element.17.terms_ref), custom_call_target="tpu_custom_call" | custom-call | tf_op jit(solution)/shard_map/sum_terms/pallas_call | solution.py:267
  123.2 41.0 %exchange_3.1 = (f32[8,2,96,256]{3,2,1,0:T(8,128)}, f32[4,2,192,256]{3,2,1,0:T(8,128)}) custom-call(f32[16,96,256]{2,1,0:T(8,128)} %sum_terms.2.rows, f32[8,192,256]{2,1,0:T(8,128)} %sum_terms.3.cols), custom_call_target="tpu_custom_call" | custom-call | tf_op jit(solution)/shard_map/exchange_3/pallas_call | solution.py:75
  164.2 2.7 %constant_dynamic-slice_fusion.omega_ref = f32[2,768,256]{2,1,0:T(8,128)} fusion(f32[8,768,256]{2,1,0:T(8,128)} %omega_ref.1, s32[]{:T(128)S(6)} %select_n.4), kind=kLoop, calls=%fused_computation.4 | loop fusion | bytes 3145732 | tf_op jit(solution)/shard_map/dynamic_slice | solution.py:412
  166.9 0.0 copy-done
  166.9 1.2 copy.21.weight_ref
  168.1 41.1 %basis.1 = (f32[2,768,256]{2,1,0:T(8,128)}, f32[2,768,256]{2,1,0:T(8,128)}) custom-call(f32[8,2,96,256]{3,2,1,0:T(8,128)} %get-tuple-element.19.row_terms, f32[4,2,192,256]{3,2,1,0:T(8,128)} %get-tuple-element.20.col_terms, f32[2,768,256]{2,1,0:T(8,128)} %constant_dynamic-slice_fusion.omega_ref, f32[2,768,256]{2,1,0:T(8,128)} %get-tuple-element.21.psi_ref, ...), custom_call_target="tpu_custom_call" | custom-call | tf_op jit(solution)/shard_map/basis/pallas_call | solution.py:415
  209.2 46.6 %exchange_4.1 = (f32[16,96,256]{2,1,0:T(8,128)}, f32[8,192,256]{2,1,0:T(8,128)}) custom-call(f32[2,768,256]{2,1,0:T(8,128)} %get-tuple-element.22.rows, f32[2,768,256]{2,1,0:T(8,128)} %get-tuple-element.23.cols), custom_call_target="tpu_custom_call" | custom-call | tf_op jit(solution)/shard_map/exchange_4/pallas_call | solution.py:75
  255.8 0.0 copy-start.1
  255.8 2.8 %copy.25 = f32[16,96,256]{2,1,0:T(8,128)} copy(f32[16,96,256]{2,1,0:T(8,128)} %get-tuple-element.26) | data formatting | bytes 3145728
  258.6 0.0 copy-done.1
  258.6 1.1 copy.26
  (2 shorter events, 0.0 us)
Async XLA Ops:
  0.6 166.2 %copy-start = (f32[8,768]{1,0:T(8,128)S(1)}, f32[8,768]{1,0:T(8,128)}, u32[]{:S(2)}) copy-start(f32[8,768]{1,0:T(8,128)} %param.8) | copy-start | bytes 73732
  255.8 2.8 %copy-start.1 = (f32[8,192,256]{2,1,0:T(8,128)S(1)}, f32[8,192,256]{2,1,0:T(8,128)}, u32[]{:S(2)}) copy-start(f32[8,192,256]{2,1,0:T(8,128)} %get-tuple-element.27) | copy-start | bytes 4718596

commit v2 on v1

--- a/solution.py
+++ b/solution.py
@@ -1,4 +1,5 @@
 import functools
+import math
 
 import jax
 import jax.numpy as jnp
@@ -97,53 +98,45 @@
     col = lax.axis_index("col")
     yes = jnp.bool_(True)
     outgoing, incoming = [], []
-    owner_here = col // ratio == row
     for c in range(n_col):
-        outgoing.append((points_ref, out_points.at[lax.rem(col, ratio)], (row, c), lax.rem(col, ratio), owner_here))
-    for x in range(ratio):
-        incoming.append((out_points.at[x], (row, row * ratio + x), x, yes))
+        outgoing.append((points_ref, out_points.at[col], (row, c), col, yes))
+        incoming.append((out_points.at[c], (row, c), c, yes))
     for q in range(n_col):
         outgoing.append(
-            (meta_ref, out_meta.at[col], (q // ratio, row * ratio + q % ratio), ratio + col, yes)
-        )
-        incoming.append((out_meta.at[q], (col // ratio, q), ratio + q, yes))
+            (meta_ref, out_meta.at[col], (q // ratio, row * ratio + q % ratio), n_col + col, yes)
+        )
+        incoming.append((out_meta.at[q], (col // ratio, q), n_col + q, yes))
     for p in range(n_row):
-        outgoing.append((meta_ref, out_meta.at[n_col + row], (p, col), ratio + n_col + row, yes))
-        incoming.append((out_meta.at[n_col + p], (p, col), ratio + n_col + p, yes))
+        outgoing.append((meta_ref, out_meta.at[n_col + row], (p, col), 2 * n_col + row, yes))
+        incoming.append((out_meta.at[n_col + p], (p, col), 2 * n_col + p, yes))
     exchange(outgoing, incoming, pltpu.get_barrier_semaphore(), send_sem, recv_sem, local_sem)
 
 
-def spread_kernel(
-    sizes, row_terms, col_terms, psi, out_rows, out_cols, out_psi, send_sem, recv_sem, local_sem
-):
+def spread_kernel(sizes, row_terms, col_terms, out_rows, out_cols, send_sem, recv_sem, local_sem):
     n_row, n_col, ratio, own = sizes
     row = lax.axis_index("row")
     col = lax.axis_index("col")
     yes = jnp.bool_(True)
-    row_part = row_terms.shape[1] // n_col
-    col_part = col_terms.shape[1] // n_row
+    row_part = out_rows.shape[2]
+    col_part = out_cols.shape[2]
     outgoing, incoming = [], []
-    for q in range(n_col):
+    for c in range(n_col):
+        x = c % ratio
         outgoing.append(
             (
-                row_terms.at[:, q * row_part : (q + 1) * row_part],
+                row_terms.at[c // ratio, :, x * row_part : (x + 1) * row_part],
                 out_rows.at[col],
-                (q // ratio, row * ratio + q % ratio),
+                (row, c),
                 col,
                 yes,
             )
         )
-        incoming.append((out_rows.at[q], (col // ratio, q), q, yes))
+        incoming.append((out_rows.at[c], (row, c), c, yes))
     for p in range(n_row):
         outgoing.append(
             (col_terms.at[:, p * col_part : (p + 1) * col_part], out_cols.at[row], (p, col), n_col + row, yes)
         )
         incoming.append((out_cols.at[p], (p, col), n_col + p, yes))
-    has_psi = col // ratio == row
-    first = lax.rem(col, ratio) * (own * n_row)
-    for p in range(n_row):
-        outgoing.append((psi.at[pl.ds(first + p * own, own)], out_psi, (p, col), n_col + n_row, has_psi))
-    incoming.append((out_psi, (col // ratio, col), n_col + n_row, yes))
     exchange(outgoing, incoming, pltpu.get_barrier_semaphore(), send_sem, recv_sem, local_sem)
 
 
@@ -208,24 +201,70 @@
     )
 
 
-def terms_kernel(pairs, left_ref, right_ref, omega_ref, psi_ref, row_ref, col_ref):
-    slot = pl.program_id(0)
-    live = pairs[slot, 0] >= 0
-    zones = right_ref.shape[2]
+def upright(line):
+    size = line.shape[1]
+    return jnp.transpose(jnp.broadcast_to(line, (size, size)))
+
+
+def shape_of(left, right_ref):
+    offs = [left[n] - right_ref[n : n + 1, :] for n in range(3)]
+    spread = (offs[0] * offs[0] + offs[1] * offs[1] + offs[2] * offs[2]) + 1.0
+    inverse = lax.rsqrt(spread)
+    nx, ny, nz = [o * inverse for o in offs]
+    weight = COUPLE * inverse * inverse * inverse * left[3] * right_ref[3:4, :]
+    u = [nx * nx, ny * ny, nz * nz, ROOT_TWO * ny * nz, ROOT_TWO * nx * nz, ROOT_TWO * nx * ny]
+    return u, weight
+
+
+def row_terms_kernel(ids, left_ref, right_ref, omega_ref, out_ref, held):
+    n = pl.program_id(0)
+    live = ids[n, 0] >= 0
+    slab = ids[n, 2]
+    zones = right_ref.shape[1]
+    rows = out_ref.shape[1]
+    step = math.gcd(zones, rows)
+    per = zones // step
 
     @pl.when(jnp.logical_not(live))
     def _():
-        row_ref[...] = jnp.zeros_like(row_ref)
-        col_ref[...] = jnp.zeros_like(col_ref)
+        out_ref[...] = jnp.zeros_like(out_ref)
 
     @pl.when(live)
     def _():
-        offs = [left_ref[0, :, n : n + 1] - right_ref[0, n : n + 1, :] for n in range(3)]
-        spread = (offs[0] * offs[0] + offs[1] * offs[1] + offs[2] * offs[2]) + 1.0
-        inverse = lax.rsqrt(spread)
-        nx, ny, nz = [o * inverse for o in offs]
-        weight = COUPLE * inverse * inverse * inverse * left_ref[0, :, 3:4] * right_ref[0, 3:4, :]
-        u = [nx * nx, ny * ny, nz * nz, ROOT_TWO * ny * nz, ROOT_TWO * nx * nz, ROOT_TWO * nx * ny]
+        for m in range(4):
+            held[m] = upright(left_ref[0, m : m + 1, :])
+        for g in range(rows // step):
+            which = slab * (rows // step) + g
+            p = which // per
+            start = pl.multiple_of((which % per) * step, step)
+            u, weight = shape_of([held[m, pl.ds(start, step), :] for m in range(4)], right_ref)
+            mine = u[5]
+            for k in range(5):
+                mine = jnp.where(p == k, u[k], mine)
+            trace = (p < 3).astype(jnp.float32)
+            parts = []
+            for q in range(6):
+                val = trace * u[q] - 5.0 * mine * u[q] + (p == q).astype(jnp.float32)
+                if q < 3:
+                    val = val + mine
+                parts.append(weight * val)
+            strip = jnp.concatenate(parts, axis=1)
+            out_ref[0, g * step : (g + 1) * step, :] = dot(strip, omega_ref[0], ((1,), (0,)))
+
+
+def col_terms_kernel(ids, left_ref, right_ref, psi_ref, out_ref):
+    n = pl.program_id(0)
+    live = ids[n, 0] >= 0
+    zones = right_ref.shape[1]
+
+    @pl.when(jnp.logical_not(live))
+    def _():
+        out_ref[...] = jnp.zeros_like(out_ref)
+
+    @pl.when(live)
+    def _():
+        left = [upright(right_ref[m : m + 1, :]) for m in range(4)]
+        u, weight = shape_of(left, left_ref.at[0])
         for p in range(6):
             parts = []
             for q in range(6):
@@ -238,43 +277,33 @@
                     val = val + 1.0
                 parts.append(weight * val)
             strip = jnp.concatenate(parts, axis=1)
-            span = slice(p * zones, (p + 1) * zones)
-            row_ref[0, span, :] = dot(strip, omega_ref[0], ((1,), (0,)))
-            term = dot(strip, psi_ref[0, span, :], ((0,), (0,)))
-            if p == 0:
-                col_ref[0] = term
-            else:
-                col_ref[0] += term
-
-
-def add_kernel(ids, terms_ref, out_ref):
-    count = terms_ref.shape[0]
-    slots = terms_ref.shape[1]
-    out_ref[...] = jnp.zeros_like(out_ref)
-
-    @pl.loop(0, count * slots)
-    def _(n):
-        target = ids[n]
-
-        @pl.when(target >= 0)
-        def _():
-            out_ref[target] += terms_ref[n // slots, n % slots]
-
-
-def sum_terms(terms, ids, clusters):
-    part = terms.shape[2]
-    width = terms.shape[3]
+            out_ref[0, p * zones : (p + 1) * zones, :] = dot(strip, psi_ref[0], ((1,), (0,)))
+
+
+def add_kernel(row_ids, col_ids, rows_ref, cols_ref, out_rows, out_cols):
+    for ids, terms_ref, out_ref in ((row_ids, rows_ref, out_rows), (col_ids, cols_ref, out_cols)):
+        out_ref[...] = jnp.zeros_like(out_ref)
+        slots = terms_ref.shape[1]
+
+        @pl.loop(0, terms_ref.shape[0] * slots)
+        def _(n):
+            target = ids[n]
+
+            @pl.when(target >= 0)
+            def _():
+                out_ref[target] += terms_ref[n // slots, n % slots]
+
+
+def sum_terms(row_ids, col_ids, rows, cols, row_clusters, col_clusters):
+    whole = pl.BlockSpec(memory_space=pltpu.VMEM)
+    table = pl.BlockSpec(memory_space=pltpu.SMEM)
     return pl.pallas_call(
         add_kernel,
-        out_shape=f32(clusters, part, width),
-        grid_spec=pltpu.PrefetchScalarGridSpec(
-            num_scalar_prefetch=1,
-            grid=(1,),
-            in_specs=[pl.BlockSpec(terms.shape, lambda n, _: (0, 0, 0, 0), pipeline_mode=pl.Buffered(1))],
-            out_specs=pl.BlockSpec((clusters, part, width), lambda n, _: (0, 0, 0), pipeline_mode=pl.Buffered(1)),
-        ),
+        out_shape=[f32(row_clusters, *rows.shape[2:]), f32(col_clusters, *cols.shape[2:])],
+        in_specs=[table, table, whole, whole],
+        out_specs=[whole, whole],
         name="sum_terms",
-    )(ids, terms)
+    )(row_ids, col_ids, rows, cols)
 
 
 def invert_base(blocks):
@@ -304,15 +333,25 @@
     return [jnp.concatenate(d, axis=0) for d in done]
 
 
-def basis_kernel(own, row_terms, col_terms, omega_ref, psi_ref, weight_ref, row_ref, col_ref, aug):
+def basis_kernel(
+    own, place, row_terms, col_terms, omega_ref, psi_ref, weight_ref, row_ref, col_ref, aug
+):
     width = omega_ref.shape[2]
+    height = omega_ref.shape[1]
     for k in range(own):
-        for terms, start, out in ((row_terms, omega_ref, row_ref), (col_terms, psi_ref, col_ref)):
-            pieces = terms.shape[0]
+        scale = weight_ref[pl.ds(place[0] * own + k, 1), :]
+        for p in range(height // LANES):
+            span = slice(p * LANES, (p + 1) * LANES)
+            tile = upright(scale[:, span])
+            for half in range(width // LANES):
+                lanes = slice(half * LANES, (half + 1) * LANES)
+                row_ref[k, span, lanes] = tile * omega_ref[k, span, lanes]
+                col_ref[k, span, lanes] = tile * psi_ref[k, span, lanes]
+        for terms, out in ((row_terms, row_ref), (col_terms, col_ref)):
             part = terms.shape[2]
-            for c in range(pieces):
+            for c in range(terms.shape[0]):
                 span = slice(c * part, (c + 1) * part)
-                out[k, span, :] = weight_ref[k, span, :] * start[k, span, :] + terms[c, k]
+                out[k, span, :] += terms[c, k]
     rows = lax.broadcasted_iota(jnp.int32, (width, width), 0)
     cols = lax.broadcasted_iota(jnp.int32, (width, width), 1)
     eye = (rows == cols).astype(jnp.float32)
@@ -336,6 +375,22 @@
         out[k] = dot(out[k], aug[m, :, width:], ((1,), (1,)))
 
 
+def move_psi(psi, own, ratio, row, col, n_row, n_col):
+    first = lax.rem(col, ratio) * (own * n_row)
+    result = None
+    home = col // ratio
+    for shift in range(n_row):
+        target = lax.rem(home + shift, n_row)
+        piece = lax.dynamic_slice_in_dim(psi, first + target * own, own, 0)
+        if shift:
+            pairs = [
+                ((c // ratio) * n_col + c, ((c // ratio + shift) % n_row) * n_col + c) for c in range(n_col)
+            ]
+            piece = lax.ppermute(piece, ("row", "col"), pairs)
+        result = piece if result is None else jnp.where(row == target, piece, result)
+    return result
+
+
 def per_device(positions, modulus, self_weight, omega, psi, blocks, *, n_row, n_col):
     col_clusters, height, width = omega.shape
     row_clusters = psi.shape[0]
@@ -346,61 +401,84 @@
     col = lax.axis_index("col")
     pairs = blocks.reshape(-1, 2)
     slots = pairs.shape[0]
+    own_psi = move_psi(psi, own, ratio, row, col, n_row, n_col)
 
     points = jnp.concatenate([positions, modulus[None]], axis=0)
     meta = jnp.pad(pairs.astype(jnp.float32).reshape(1, -1), ((0, 7), (0, LANES - 2 * slots)))
     all_points, all_meta = remote_call(
         functools.partial(gather_kernel, (n_row, n_col, ratio)),
-        [f32(ratio, 4, positions.shape[1]), f32(n_col + n_row, 8, LANES)],
+        [f32(n_col, 4, positions.shape[1]), f32(n_col + n_row, 8, LANES)],
         2 * n_col + n_row,
-        ratio + n_col + n_row,
+        2 * n_col + n_row,
         1,
         [points, meta],
     )
-    row_points = all_points.reshape(ratio, 4, col_clusters, zones).transpose(0, 2, 3, 1)
-    row_points = row_points.reshape(row_clusters, zones, 4)
-    col_points = points.reshape(4, col_clusters, zones).transpose(1, 0, 2)
     metas = all_meta[:, 0, : 2 * slots].astype(jnp.int32).reshape(n_col + n_row, slots, 2)
     row_ids = metas[:n_col, :, 0].reshape(-1)
     col_ids = metas[n_col:, :, 1].reshape(-1)
 
-    row_terms, col_terms = pl.pallas_call(
-        terms_kernel,
-        out_shape=[f32(slots, height, width), f32(slots, height, width)],
-        grid_spec=pltpu.PrefetchScalarGridSpec(
-            num_scalar_prefetch=1,
-            grid=(slots,),
-            in_specs=[
-                pl.BlockSpec((1, zones, 4), lambda n, ids: (jnp.maximum(ids[n, 0], 0), 0, 0)),
-                pl.BlockSpec((1, 4, zones), lambda n, ids: (jnp.maximum(ids[n, 1], 0), 0, 0)),
-                pl.BlockSpec((1, height, width), lambda n, ids: (jnp.maximum(ids[n, 1], 0), 0, 0)),
-                pl.BlockSpec((1, height, width), lambda n, ids: (jnp.maximum(ids[n, 0], 0), 0, 0)),
-            ],
-            out_specs=[
-                pl.BlockSpec((1, height, width), lambda n, ids: (n, 0, 0)),
-                pl.BlockSpec((1, height, width), lambda n, ids: (n, 0, 0)),
-            ],
-        ),
-        name="terms",
-    )(pairs, row_points, col_points, omega, psi)
+    def table(lefts, rights, base, extra):
+        at = jnp.where(lefts >= 0, lefts + base, -1)
+        return jnp.stack([at, rights, jnp.broadcast_to(extra, at.shape)], axis=-1)
+
+    row_base = (jnp.arange(n_row * slots, dtype=jnp.int32) // slots) * row_clusters
+    row_table = table(metas[n_col:, :, 0].reshape(-1), col_ids, row_base, row)
+    col_table = table(pairs[:, 0], pairs[:, 1], row * row_clusters, row)
+
+    def left_map(n, ids):
+        at = jnp.maximum(ids[n, 0], 0)
+        return (at // col_clusters, 0, at % col_clusters)
+
+    def term_call(kernel, count, rows, clusters_map, scratch, name):
+        return pl.pallas_call(
+            kernel,
+            out_shape=f32(count, rows, width),
+            grid_spec=pltpu.PrefetchScalarGridSpec(
+                num_scalar_prefetch=1,
+                grid=(count,),
+                in_specs=[
+                    pl.BlockSpec((1, 4, zones), left_map),
+                    pl.BlockSpec((4, zones), lambda n, ids: (0, jnp.maximum(ids[n, 1], 0))),
+                    pl.BlockSpec((1, height, width), clusters_map),
+                ],
+                out_specs=pl.BlockSpec((1, rows, width), lambda n, ids: (n, 0, 0)),
+                scratch_shapes=scratch,
+            ),
+            cost_estimate=pl.CostEstimate(
+                flops=12 * count * rows * height * width, bytes_accessed=8 * count * height * width, transcendentals=0
+            ),
+            name=name,
+        )
+
+    row_terms = term_call(
+        row_terms_kernel,
+        n_row * slots,
+        height // n_row,
+        lambda n, ids: (jnp.maximum(ids[n, 1], 0), 0, 0),
+        [pltpu.VMEM((4, zones, zones), jnp.float32)],
+        "row_terms",
+    )(row_table, all_points, points, omega)
+    col_terms = term_call(
+        col_terms_kernel,
+        slots,
+        height,
+        lambda n, ids: (lax.rem(jnp.maximum(ids[n, 0], 0), row_clusters), 0, 0),
+        [],
+        "col_terms",
+    )(col_table, all_points, points, psi)
 
     sizes = (n_row, n_col, ratio, own)
     row_part = height // n_col
     col_part = height // n_row
-    got_rows, got_cols, own_psi = remote_call(
+    got_rows, got_cols = remote_call(
         functools.partial(spread_kernel, sizes),
-        [
-            f32(n_col, slots, row_part, width),
-            f32(n_row, slots, col_part, width),
-            f32(own, height, width),
-        ],
-        n_col + 2 * n_row,
-        n_col + n_row + 1,
+        [f32(n_col, slots, row_part, width), f32(n_row, slots, col_part, width)],
+        n_col + n_row,
+        n_col + n_row,
         2,
-        [row_terms, col_terms, psi],
-    )
-    row_chunks = sum_terms(got_rows, row_ids, row_clusters)
-    col_chunks = sum_terms(got_cols, col_ids, col_clusters)
+        [row_terms.reshape(n_row, slots, height // n_row, width), col_terms],
+    )
+    row_chunks, col_chunks = sum_terms(row_ids, col_ids, got_rows, got_cols, row_clusters, col_clusters)
     full_rows, full_cols = remote_call(
         functools.partial(collect_kernel, sizes),
         [f32(n_col, own, row_part, width), f32(n_row, own, col_part, width)],
@@ -409,17 +487,28 @@
         3,
         [row_chunks, col_chunks],
     )
-    own_omega = lax.dynamic_slice_in_dim(omega, row * own, own, 0)
-    own_weight = lax.dynamic_slice_in_dim(self_weight, row * own, own, 0)[:, :, None]
-    full = pl.BlockSpec(memory_space=pltpu.VMEM)
+
+    def whole(shape):
+        return pl.BlockSpec(shape, lambda n, _: (0,) * len(shape), pipeline_mode=pl.Buffered(1))
+
     row_basis, col_basis = pl.pallas_call(
         functools.partial(basis_kernel, own),
         out_shape=[f32(own, height, width), f32(own, height, width)],
-        in_specs=[full] * 5,
-        out_specs=[full] * 2,
-        scratch_shapes=[pltpu.VMEM((2 * own, width, 2 * width), jnp.float32)],
+        grid_spec=pltpu.PrefetchScalarGridSpec(
+            num_scalar_prefetch=1,
+            grid=(1,),
+            in_specs=[
+                whole(full_rows.shape),
+                whole(full_cols.shape),
+                pl.BlockSpec((own, height, width), lambda n, at: (at[0], 0, 0), pipeline_mode=pl.Buffered(1)),
+                whole(own_psi.shape),
+                whole(self_weight.shape),
+            ],
+            out_specs=[whole(own_psi.shape), whole(own_psi.shape)],
+            scratch_shapes=[pltpu.VMEM((2 * own, width, 2 * width), jnp.float32)],
+        ),
         name="basis",
-    )(full_rows, full_cols, own_omega, own_psi, own_weight)
+    )(row.astype(jnp.int32)[None], full_rows, full_cols, omega, own_psi, self_weight)
     return tuple(
         remote_call(
             functools.partial(deliver_kernel, sizes),

time: 262 us -> 250 us (0.954)
  Pallas kernels: 243 us -> 228 us
  starting transfers between devices: 0 us -> 4.93 us
    pallas_call x4, Pallas kernels: 185 us -> 162 us  [remote_call(): pl.pallas_call(body, out_shape=out_shapes, in_specs=[ANY] * len(operands)...]
    pallas_call x3, Pallas kernels: 17.1 us -> 24.2 us  [the longest x1 14.4 us: per_device(): term_call(row_terms_kernel, n_row * slots, height // n_row, lambda n, ids...]
    ppermute x0 -> x3, starting transfers between devices: none -> 4.93 us  [move_psi(): piece = lax.ppermute(piece, ('row', 'col'), pairs)]
    select_n x0 -> x3, other arithmetic: none -> 3.53 us  [the longest x1 3.44 us: move_psi(): jnp.where(row == target, piece, result)]
  transfers between devices with their start and end apart: 0 -> 3, of which waited for: 0 -> 0; matrix products, arithmetic and copies ran while one was open for 0% -> 2% of each run, Pallas kernels for 0% -> 55%
where the time goes in v2:
time: 250 us
  Pallas kernels  228 us (91%)
  local copies, waits for them, and re-layouts  10.5 us (4%)
  other arithmetic  6.25 us (2%)
  starting transfers between devices  4.93 us (2%)
    pallas_call x4, Pallas kernels, remote_call(): pl.pallas_call(body, out_shape=out_shapes, in_specs=[ANY] * len(operands)...  162 us
    pallas_call x1, Pallas kernels, per_device(): pl.pallas_call(functools.partial(basis_kernel, own), out_shape=[f32(own,...  41.2 us
    pallas_call x1, Pallas kernels, per_device(): term_call(row_terms_kernel, n_row * slots, height // n_row, lambda n, ids...  14.4 us
    pallas_call x1, Pallas kernels, per_device(): term_call(col_terms_kernel, slots, height, lambda n, ids: (lax.rem(jnp.ma...  5.47 us
  transfers between devices with their start and end apart: 3, of which 0 were waited for; matrix products, arithmetic and copies ran while one was open for 2% of the time, Pallas kernels for 55%

profile of v2, /device:TPU:27, one launch (start us, length us, event | category | flops | bytes accessed | tf_op | source)
XLA Modules:
  0.0 250.3 jit_solution(643726447582047050)
XLA Ops:
  0.7 0.0 copy-start.2
  0.7 0.0 copy-start.1
  0.7 0.0 copy-start.3
  0.7 3.9 %constant_dynamic-slice_fusion = (f32[2,768,256]{2,1,0:T(8,128)S(1)}, f32[2,768,256]{2,1,0:T(8,128)S(1)}, f32[2,768,256]{2,1,0:T(8,128)}) fusion(f32[16,768,256]{2,1,0:T(8,128)} %psi_ref.1, s32[]{:T(128)S(6)} %select_n.74, s32[]{:T(128)S(6)} %select_n.72, s32[]{:T(128)S(6)} %select_n.70), kind=kLoop, calls=%fused_computation.16 | loop fusion | bytes 9437196 | tf_op jit(solution)/shard_map/dynamic_slice | solution.py:384
  4.7 1.8 collective-permute-start
  6.4 1.3 collective-permute-start.1
  7.7 1.9 collective-permute-start.2
  9.6 0.0 copy-done.2
  9.6 0.1 convert_element_type.23
  9.7 0.0 copy-done.1
  9.7 0.0 copy-done.3
  9.7 0.6 pad_maximum_fusion.points_ref.right_ref
  10.3 0.6 pad.4.meta_ref
  10.9 36.4 %exchange_1.1 = (f32[8,4,1024]{2,1,0:T(4,128)}, f32[12,8,128]{2,1,0:T(8,128)}) custom-call(f32[4,1024]{1,0:T(4,128)} %pad_maximum_fusion.points_ref.right_ref, f32[8,128]{1,0:T(8,128)} %pad.4.meta_ref), custom_call_target="tpu_custom_call" | custom-call | tf_op jit(solution)/shard_map/exchange_1/pallas_call | solution.py:76
  47.3 0.8 slice_convert_fusion
  48.1 0.1 copy.24
  48.2 0.1 fusion.6
  48.3 0.1 copy.26
  48.4 0.1 stack_reshape_squeeze.4
  48.5 0.6 reshape_squeeze.10.col_ids
  49.1 0.1 pad.10.clone
  49.1 0.1 copy.27
  49.2 0.1 reshape_squeeze.12
  49.3 0.1 copy.25
  49.4 0.6 reshape_squeeze.9.row_ids
  50.0 0.1 compare_select_fusion
  50.1 0.6 add_add_fusion.1.ids
  50.8 0.7 add_add_fusion.ids
  51.4 5.5 %col_terms.1 = f32[2,768,256]{2,1,0:T(8,128)} custom-call(s32[2,3]{1,0:T(2,128)} %add_add_fusion.1.ids, f32[8,4,1024]{2,1,0:T(4,128)} %get-tuple-element.13.left_ref, f32[4,1024]{1,0:T(4,128)} %pad_maximum_fusion.points_ref.right_ref, f32[16,768,256]{2,1,0:T(8,128)} %psi_ref.1), custom_call_target="tpu_custom_call" | custom-call | flops 3623878656 | bytes 3145728 | tf_op jit(solution)/shard_map/col_terms/pallas_call | solution.py:461
  56.9 14.4 %row_terms.1 = f32[8,192,256]{2,1,0:T(8,128)} custom-call(s32[8,3]{1,0:T(8,128)} %add_add_fusion.ids, f32[8,4,1024]{2,1,0:T(4,128)} %get-tuple-element.13.left_ref, f32[4,1024]{1,0:T(4,128)} %pad_maximum_fusion.points_ref.right_ref, f32[8,768,256]{2,1,0:T(8,128)} %omega_ref.3), custom_call_target="tpu_custom_call" | custom-call | flops 3623878656 | bytes 12582912 | tf_op jit(solution)/shard_map/row_terms/pallas_call | solution.py:453
  71.3 39.4 %exchange_2.1 = (f32[8,2,96,256]{3,2,1,0:T(8,128)}, f32[4,2,192,256]{3,2,1,0:T(8,128)}) custom-call(f32[4,2,192,256]{3,2,1,0:T(8,128)} %bitcast.15, f32[2,768,256]{2,1,0:T(8,128)} %col_terms.1), custom_call_target="tpu_custom_call" | custom-call | tf_op jit(solution)/shard_map/exchange_2/pallas_call | solution.py:76
  110.7 4.3 %sum_terms.1 = (f32[16,96,256]{2,1,0:T(8,128)}, f32[8,192,256]{2,1,0:T(8,128)}) custom-call(s32[16]{0:T(128)} %reshape_squeeze.9.row_ids, s32[8]{0:T(128)} %reshape_squeeze.10.col_ids, f32[8,2,96,256]{3,2,1,0:T(8,128)} %get-tuple-element.14.rows_ref, f32[4,2,192,256]{3,2,1,0:T(8,128)} %get-tuple-element.15.cols_ref), custom_call_target="tpu_custom_call" | custom-call | tf_op jit(solution)/shard_map/sum_terms/pallas_call | solution.py:300
  115.1 36.8 %exchange_3.1 = (f32[8,2,96,256]{3,2,1,0:T(8,128)}, f32[4,2,192,256]{3,2,1,0:T(8,128)}) custom-call(f32[16,96,256]{2,1,0:T(8,128)} %get-tuple-element.16.rows, f32[8,192,256]{2,1,0:T(8,128)} %get-tuple-element.17.cols), custom_call_target="tpu_custom_call" | custom-call | tf_op jit(solution)/shard_map/exchange_3/pallas_call | solution.py:76
  151.9 0.0 collective-permute-done
  151.9 0.0 collective-permute-done.1
  151.9 0.0 collective-permute-done.2
  151.9 3.4 %select_select_fusion.psi_ref = f32[2,768,256]{2,1,0:T(8,128)} fusion(f32[2,768,256]{2,1,0:T(8,128)} %collective-permute-done, f32[2,768,256]{2,1,0:T(8,128)} %collective-permute-done.1, f32[2,768,256]{2,1,0:T(8,128)} %collective-permute-done.2, f32[16,768,256]{2,1,0:T(8,128)} %psi_ref.1, s32[]{:T(128)S(6)} %select_n.75, pred[]{:T(512)S(6)} %eq.11, ...), kind=kLoop, calls=%fused_computation | loop fusion | flops 1179648 | bytes 7864327 | tf_op jit(solution)/shard_map/jit(_where)/select_n | solution.py:390
  155.4 41.2 %basis.1 = (f32[2,768,256]{2,1,0:T(8,128)}, f32[2,768,256]{2,1,0:T(8,128)}) custom-call(s32[1]{0:T(128)} %bitcast.place, f32[8,2,96,256]{3,2,1,0:T(8,128)} %get-tuple-element.18.row_terms, f32[4,2,192,256]{3,2,1,0:T(8,128)} %get-tuple-element.19.col_terms, f32[8,768,256]{2,1,0:T(8,128)} %omega_ref.3, f32[2,768,256]{2,1,0:T(8,128)} %select_select_fusion.psi_ref, ...), custom_call_target="tpu_custom_call" | custom-call | tf_op jit(solution)/shard_map/basis/pallas_call | solution.py:494
  196.5 49.8 %exchange_4.1 = (f32[16,96,256]{2,1,0:T(8,128)}, f32[8,192,256]{2,1,0:T(8,128)}) custom-call(f32[2,768,256]{2,1,0:T(8,128)} %get-tuple-element.20.rows, f32[2,768,256]{2,1,0:T(8,128)} %get-tuple-element.21.cols), custom_call_target="tpu_custom_call" | custom-call | tf_op jit(solution)/shard_map/exchange_4/pallas_call | solution.py:76
  246.3 0.0 copy-start
  246.4 2.8 %copy.34 = f32[16,96,256]{2,1,0:T(8,128)} copy(f32[16,96,256]{2,1,0:T(8,128)} %get-tuple-element.31) | data formatting | bytes 3145728
  249.2 0.0 copy-done
  249.2 1.1 copy.35
  (3 shorter events, 0.0 us)
Async XLA Ops:
  0.7 8.9 %copy-start.2 = (s32[1,1,2,2]{3,2,1,0:T(2,128)S(1)}, s32[1,1,2,2]{3,2,1,0:T(2,128)}, u32[]{:S(2)}) copy-start(s32[1,1,2,2]{3,2,1,0:T(2,128)} %param.11) | copy-start | bytes 52
  0.7 9.0 %copy-start.1 = (f32[3,1024]{1,0:T(4,128)S(1)}, f32[3,1024]{1,0:T(4,128)}, u32[]{:S(2)}) copy-start(f32[3,1024]{1,0:T(4,128)} %param.6) | copy-start | bytes 36868
  0.7 9.0 %copy-start.3 = (f32[1024]{0:T(1024)S(1)}, f32[1024]{0:T(1024)}, u32[]{:S(2)}) copy-start(f32[1024]{0:T(1024)} %param.7) | copy-start | bytes 12292
  4.7 147.2 %collective-permute-start = (f32[2,768,256]{2,1,0:T(8,128)}, f32[2,768,256]{2,1,0:T(8,128)}, u32[]{:S(2)}, u32[]{:S(2)}) collective-permute-start(f32[2,768,256]{2,1,0:T(8,128)} %get-tuple-element.24), channel_id=1, source_target_pairs={{0,24},{1,25},{10,2},{11,3},{20,12},{21,13},{30,22},{31,23}} | collective-permute-start | bytes 4718600 | tf_op jit(solution)/shard_map/ppermute | solution.py:389
  6.4 145.5 %collective-permute-start.1 = (f32[2,768,256]{2,1,0:T(8,128)S(1)}, f32[2,768,256]{2,1,0:T(8,128)}, u32[]{:S(2)}, u32[]{:S(2)}) collective-permute-start(f32[2,768,256]{2,1,0:T(8,128)S(1)} %get-tuple-element.23), channel_id=1, source_target_pairs={{0,16},{1,17},{10,26},{11,27},{20,4},{21,5},{30,14},{31,15}} | collective-permute-start | bytes 4718600 | tf_op jit(solution)/shard_map/ppermute | solution.py:389
  7.7 144.2 %collective-permute-start.2 = (f32[2,768,256]{2,1,0:T(8,128)S(1)}, f32[2,768,256]{2,1,0:T(8,128)}, u32[]{:S(2)}, u32[]{:S(2)}) collective-permute-start(f32[2,768,256]{2,1,0:T(8,128)S(1)} %get-tuple-element.22), channel_id=1, source_target_pairs={{0,8},{1,9},{10,18},{11,19},{20,28},{21,29},{30,6},{31,7}} | collective-permute-start | bytes 4718600 | tf_op jit(solution)/shard_map/ppermute | solution.py:389
  246.3 2.8 %copy-start = (f32[8,192,256]{2,1,0:T(8,128)S(1)}, f32[8,192,256]{2,1,0:T(8,128)}, u32[]{:S(2)}) copy-start(f32[8,192,256]{2,1,0:T(8,128)} %get-tuple-element.32) | copy-start | bytes 4718596

commit v3 on v2

--- a/solution.py
+++ b/solution.py
@@ -12,6 +12,7 @@
 ROOT_TWO = 1.4142135623730951
 HIGH = lax.Precision.HIGHEST
 BASE = 64
+GROUP = 4
 LANES = 128
 MESH = pl.DeviceIdType.MESH
 ANY = pl.BlockSpec(memory_space=pl.ANY)
@@ -308,29 +309,48 @@
 
 def invert_base(blocks):
     size = blocks[0].shape[0]
+    wide = (8, 2 * size)
     rows = lax.broadcasted_iota(jnp.int32, (size, size), 0)
     cols = lax.broadcasted_iota(jnp.int32, (size, size), 1)
     eye = (rows == cols).astype(jnp.float32)
-    work = [jnp.concatenate([b, eye], axis=1) for b in blocks]
+    sub = lax.broadcasted_iota(jnp.int32, wide, 0)
+    work = []
+    for b in blocks:
+        both = jnp.concatenate([b, eye], axis=1)
+        work.append([both[8 * t : 8 * t + 8] for t in range(size // 8)])
     done = [[] for _ in blocks]
-    for k in range(size):
-        low = (k // 8) * 8
-        nxt = []
-        for m, w in enumerate(work):
-            at = k - low
-            pivot_row = w[at : at + 1, :]
-            d = pivot_row[:, k : k + 1]
-            root = lax.rsqrt(d)
-            scaled = pivot_row * root
-            done[m].append(scaled[:, size:])
-            if k + 1 < size:
-                column = w[:, k : k + 1] * root
-                if at == 7:
-                    nxt.append(w[8:] - column[8:] * scaled)
-                else:
-                    nxt.append(w - column * scaled)
-        work = nxt
-    return [jnp.concatenate(d, axis=0) for d in done]
+    for k in range(0, size, GROUP):
+        first = k // 8
+        at = k % 8
+        for m, tiles in enumerate(work):
+            line = [jnp.broadcast_to(tiles[first][at + a : at + a + 1, :], wide) for a in range(GROUP)]
+            side = [
+                [jnp.broadcast_to(tiles[t][:, k + a : k + a + 1], wide) for t in range(first, size // 8)]
+                for a in range(GROUP)
+            ]
+            small = [
+                [jnp.broadcast_to(line[a][:, k + c : k + c + 1], wide) for c in range(a + 1)] for a in range(GROUP)
+            ]
+            for c in range(GROUP):
+                root = lax.rsqrt(small[c][c])
+                line[c] = line[c] * root
+                side[c] = [v * root for v in side[c]]
+                factor = [small[a][c] * root for a in range(c + 1, GROUP)]
+                for a in range(c + 1, GROUP):
+                    f = factor[a - c - 1]
+                    line[a] = line[a] - f * line[c]
+                    side[a] = [v - f * w for v, w in zip(side[a], side[c])]
+                    for e in range(c + 1, a + 1):
+                        small[a][e] = small[a][e] - f * factor[e - c - 1]
+            if at == 0:
+                done[m].append(line[0])
+            for a in range(GROUP):
+                done[m][first] = jnp.where(sub == at + a, line[a], done[m][first])
+            stay = first + (at + GROUP == 8)
+            for t in range(stay, size // 8):
+                for a in range(GROUP):
+                    tiles[t] = tiles[t] - side[a][t - first] * line[a]
+    return [jnp.concatenate(d, axis=0)[:, size:] for d in done]
 
 
 def basis_kernel(
@@ -401,7 +421,6 @@
     col = lax.axis_index("col")
     pairs = blocks.reshape(-1, 2)
     slots = pairs.shape[0]
-    own_psi = move_psi(psi, own, ratio, row, col, n_row, n_col)
 
     points = jnp.concatenate([positions, modulus[None]], axis=0)
     meta = jnp.pad(pairs.astype(jnp.float32).reshape(1, -1), ((0, 7), (0, LANES - 2 * slots)))
@@ -413,6 +432,8 @@
         1,
         [points, meta],
     )
+    all_points, all_meta, late_psi = lax.optimization_barrier((all_points, all_meta, psi))
+    own_psi = move_psi(late_psi, own, ratio, row, col, n_row, n_col)
     metas = all_meta[:, 0, : 2 * slots].astype(jnp.int32).reshape(n_col + n_row, slots, 2)
     row_ids = metas[:n_col, :, 0].reshape(-1)
     col_ids = metas[n_col:, :, 1].reshape(-1)

time: 250 us -> 224 us (0.90)
  Pallas kernels: 228 us -> 199 us
    pallas_call x4, Pallas kernels: 162 us -> 141 us  [remote_call(): pl.pallas_call(body, out_shape=out_shapes, in_specs=[ANY] * len(operands)...]
    pallas_call x1, Pallas kernels: 41.2 us -> 35.4 us  [per_device(): pl.pallas_call(functools.partial(basis_kernel, own), out_shape=[f32(own,...]
  transfers between devices with their start and end apart: 3 -> 3, of which waited for: 0 -> 0; matrix products, arithmetic and copies ran while one was open for 2% -> 2% of each run, Pallas kernels for 55% -> 46%
where the time goes in v3:
time: 224 us; the launch traced here: 223 us
  Pallas kernels  199 us (89%)
  local copies, waits for them, and re-layouts  10.5 us (5%)
  other arithmetic  7.67 us (3%)
  starting transfers between devices  4.93 us (2%)
    pallas_call x4, Pallas kernels, remote_call(): pl.pallas_call(body, out_shape=out_shapes, in_specs=[ANY] * len(operands)...  141 us
    pallas_call x1, Pallas kernels, per_device(): pl.pallas_call(functools.partial(basis_kernel, own), out_shape=[f32(own,...  35.4 us
    pallas_call x1, Pallas kernels, per_device(): term_call(row_terms_kernel, n_row * slots, height // n_row, lambda n, ids...  12.9 us
    pallas_call x1, Pallas kernels, per_device(): term_call(col_terms_kernel, slots, height, lambda n, ids: (lax.rem(jnp.ma...  5.47 us
    ppermute x3, starting transfers between devices, move_psi(): piece = lax.ppermute(piece, ('row', 'col'), pairs)  4.93 us
  transfers between devices with their start and end apart: 3, of which 0 were waited for; matrix products, arithmetic and copies ran while one was open for 2% of the time, Pallas kernels for 46%

profile of v3, /device:TPU:27, one launch (start us, length us, event | category | flops | bytes accessed | tf_op | source)
XLA Modules:
  0.0 223.0 jit_solution(7028728051487716288)
XLA Ops:
  0.7 0.7 convert_element_type.22
  1.4 0.1 convert_element_type.23
  1.5 1.3 pad_maximum_fusion.points_ref.right_ref
  2.8 0.6 pad.4.meta_ref
  3.4 9.6 %exchange_1.1 = (f32[8,4,1024]{2,1,0:T(4,128)}, f32[12,8,128]{2,1,0:T(8,128)}) custom-call(f32[4,1024]{1,0:T(4,128)} %pad_maximum_fusion.points_ref.right_ref, f32[8,128]{1,0:T(8,128)} %pad.4.meta_ref), custom_call_target="tpu_custom_call" | custom-call | tf_op jit(solution)/shard_map/exchange_1/pallas_call | solution.py:77
  13.0 0.0 copy-start.1
  13.0 3.9 %constant_dynamic-slice_fusion = (f32[2,768,256]{2,1,0:T(8,128)S(1)}, f32[2,768,256]{2,1,0:T(8,128)S(1)}, f32[2,768,256]{2,1,0:T(8,128)}) fusion(f32[16,768,256]{2,1,0:T(8,128)} %psi_ref.1, s32[]{:T(128)S(6)} %select_n.74, s32[]{:T(128)S(6)} %select_n.72, s32[]{:T(128)S(6)} %select_n.70), kind=kLoop, calls=%fused_computation.16 | loop fusion | bytes 9437196 | tf_op jit(solution)/shard_map/dynamic_slice | solution.py:404
  17.0 1.8 collective-permute-start
  18.8 1.3 collective-permute-start.1
  20.1 1.8 collective-permute-start.2
  21.9 0.8 slice_convert_fusion
  22.7 0.1 copy.24
  22.8 0.1 fusion.6
  22.9 0.1 copy.26
  23.0 0.1 stack_reshape_squeeze.4
  23.1 0.7 reshape_squeeze.10.col_ids
  23.7 0.1 copy.27
  23.8 0.1 reshape_squeeze.12
  23.9 0.1 pad.10.clone
  24.0 0.1 copy.25
  24.1 0.6 reshape_squeeze.9.row_ids
  24.7 0.0 copy-done.1
  24.7 0.1 compare_select_fusion
  24.8 0.6 add_add_fusion.1.ids
  25.4 0.7 add_add_fusion.ids
  26.1 5.5 %col_terms.1 = f32[2,768,256]{2,1,0:T(8,128)} custom-call(s32[2,3]{1,0:T(2,128)} %add_add_fusion.1.ids, f32[8,4,1024]{2,1,0:T(4,128)} %get-tuple-element.18.left_ref, f32[4,1024]{1,0:T(4,128)} %pad_maximum_fusion.points_ref.right_ref, f32[16,768,256]{2,1,0:T(8,128)} %psi_ref.1), custom_call_target="tpu_custom_call" | custom-call | flops 3623878656 | bytes 3145728 | tf_op jit(solution)/shard_map/col_terms/pallas_call | solution.py:482
  31.5 12.9 %row_terms.1 = f32[8,192,256]{2,1,0:T(8,128)} custom-call(s32[8,3]{1,0:T(8,128)} %add_add_fusion.ids, f32[8,4,1024]{2,1,0:T(4,128)} %get-tuple-element.18.left_ref, f32[4,1024]{1,0:T(4,128)} %pad_maximum_fusion.points_ref.right_ref, f32[8,768,256]{2,1,0:T(8,128)} %omega_ref.3), custom_call_target="tpu_custom_call" | custom-call | flops 3623878656 | bytes 12582912 | tf_op jit(solution)/shard_map/row_terms/pallas_call | solution.py:474
  44.4 39.1 %exchange_2.1 = (f32[8,2,96,256]{3,2,1,0:T(8,128)}, f32[4,2,192,256]{3,2,1,0:T(8,128)}) custom-call(f32[4,2,192,256]{3,2,1,0:T(8,128)} %bitcast.15, f32[2,768,256]{2,1,0:T(8,128)} %col_terms.1), custom_call_target="tpu_custom_call" | custom-call | tf_op jit(solution)/shard_map/exchange_2/pallas_call | solution.py:77
  83.6 4.3 %sum_terms.1 = (f32[16,96,256]{2,1,0:T(8,128)}, f32[8,192,256]{2,1,0:T(8,128)}) custom-call(s32[16]{0:T(128)} %reshape_squeeze.9.row_ids, s32[8]{0:T(128)} %reshape_squeeze.10.col_ids, f32[8,2,96,256]{3,2,1,0:T(8,128)} %get-tuple-element.19.rows_ref, f32[4,2,192,256]{3,2,1,0:T(8,128)} %get-tuple-element.20.cols_ref), custom_call_target="tpu_custom_call" | custom-call | tf_op jit(solution)/shard_map/sum_terms/pallas_call | solution.py:301
  87.9 40.3 %exchange_3.1 = (f32[8,2,96,256]{3,2,1,0:T(8,128)}, f32[4,2,192,256]{3,2,1,0:T(8,128)}) custom-call(f32[16,96,256]{2,1,0:T(8,128)} %get-tuple-element.21.rows, f32[8,192,256]{2,1,0:T(8,128)} %get-tuple-element.22.cols), custom_call_target="tpu_custom_call" | custom-call | tf_op jit(solution)/shard_map/exchange_3/pallas_call | solution.py:77
  128.2 0.0 collective-permute-done
  128.2 0.0 collective-permute-done.1
  128.2 0.0 collective-permute-done.2
  128.2 3.4 %select_select_fusion.psi_ref = f32[2,768,256]{2,1,0:T(8,128)} fusion(f32[2,768,256]{2,1,0:T(8,128)} %collective-permute-done, f32[2,768,256]{2,1,0:T(8,128)} %collective-permute-done.1, f32[2,768,256]{2,1,0:T(8,128)} %collective-permute-done.2, f32[16,768,256]{2,1,0:T(8,128)} %psi_ref.1, s32[]{:T(128)S(6)} %select_n.75, pred[]{:T(512)S(6)} %eq.11, ...), kind=kLoop, calls=%fused_computation | loop fusion | flops 1179648 | bytes 7864327 | tf_op jit(solution)/shard_map/jit(_where)/select_n | solution.py:410
  131.7 35.4 %basis.1 = (f32[2,768,256]{2,1,0:T(8,128)}, f32[2,768,256]{2,1,0:T(8,128)}) custom-call(s32[1]{0:T(128)} %bitcast.place, f32[8,2,96,256]{3,2,1,0:T(8,128)} %get-tuple-element.23.row_terms, f32[4,2,192,256]{3,2,1,0:T(8,128)} %get-tuple-element.24.col_terms, f32[8,768,256]{2,1,0:T(8,128)} %omega_ref.3, f32[2,768,256]{2,1,0:T(8,128)} %select_select_fusion.psi_ref, ...), custom_call_target="tpu_custom_call" | custom-call | tf_op jit(solution)/shard_map/basis/pallas_call | solution.py:515
  167.1 51.9 %exchange_4.1 = (f32[16,96,256]{2,1,0:T(8,128)}, f32[8,192,256]{2,1,0:T(8,128)}) custom-call(f32[2,768,256]{2,1,0:T(8,128)} %get-tuple-element.26.rows, f32[2,768,256]{2,1,0:T(8,128)} %get-tuple-element.27.cols), custom_call_target="tpu_custom_call" | custom-call | tf_op jit(solution)/shard_map/exchange_4/pallas_call | solution.py:77
  219.0 0.0 copy-start
  219.0 2.8 %copy.34 = f32[16,96,256]{2,1,0:T(8,128)} copy(f32[16,96,256]{2,1,0:T(8,128)} %get-tuple-element.37) | data formatting | bytes 3145728
  221.8 0.0 copy-done
  221.8 1.1 copy.35
  (2 shorter events, 0.0 us)
Async XLA Ops:
  13.0 11.7 %copy-start.1 = (s32[1,1,2,2]{3,2,1,0:T(2,128)S(1)}, s32[1,1,2,2]{3,2,1,0:T(2,128)}, u32[]{:S(2)}) copy-start(s32[1,1,2,2]{3,2,1,0:T(2,128)} %param.11) | copy-start | bytes 52
  17.0 111.2 %collective-permute-start = (f32[2,768,256]{2,1,0:T(8,128)}, f32[2,768,256]{2,1,0:T(8,128)}, u32[]{:S(2)}, u32[]{:S(2)}) collective-permute-start(f32[2,768,256]{2,1,0:T(8,128)} %get-tuple-element.30), channel_id=1, source_target_pairs={{0,24},{1,25},{10,2},{11,3},{20,12},{21,13},{30,22},{31,23}} | collective-permute-start | bytes 4718600 | tf_op jit(solution)/shard_map/ppermute | solution.py:409
  18.8 109.4 %collective-permute-start.1 = (f32[2,768,256]{2,1,0:T(8,128)S(1)}, f32[2,768,256]{2,1,0:T(8,128)}, u32[]{:S(2)}, u32[]{:S(2)}) collective-permute-start(f32[2,768,256]{2,1,0:T(8,128)S(1)} %get-tuple-element.29), channel_id=1, source_target_pairs={{0,16},{1,17},{10,26},{11,27},{20,4},{21,5},{30,14},{31,15}} | collective-permute-start | bytes 4718600 | tf_op jit(solution)/shard_map/ppermute | solution.py:409
  20.1 108.1 %collective-permute-start.2 = (f32[2,768,256]{2,1,0:T(8,128)S(1)}, f32[2,768,256]{2,1,0:T(8,128)}, u32[]{:S(2)}, u32[]{:S(2)}) collective-permute-start(f32[2,768,256]{2,1,0:T(8,128)S(1)} %get-tuple-element.28), channel_id=1, source_target_pairs={{0,8},{1,9},{10,18},{11,19},{20,28},{21,29},{30,6},{31,7}} | collective-permute-start | bytes 4718600 | tf_op jit(solution)/shard_map/ppermute | solution.py:409
  219.0 2.8 %copy-start = (f32[8,192,256]{2,1,0:T(8,128)S(1)}, f32[8,192,256]{2,1,0:T(8,128)}, u32[]{:S(2)}) copy-start(f32[8,192,256]{2,1,0:T(8,128)} %get-tuple-element.38) | copy-start | bytes 4718596

commit v4 on v3

--- a/solution.py
+++ b/solution.py
@@ -200,6 +200,16 @@
     return lax.dot_general(
         a, b, (contract, ((), ())), precision=HIGH, preferred_element_type=jnp.float32
     )
+
+
+def dot_split(a, b):
+    a_high = a.astype(jnp.bfloat16)
+    b_high = b.astype(jnp.bfloat16)
+    a_low = (a - a_high.astype(jnp.float32)).astype(jnp.bfloat16)
+    b_low = (b - b_high.astype(jnp.float32)).astype(jnp.bfloat16)
+    total = jnp.dot(a_high, b_low, preferred_element_type=jnp.float32)
+    total = total + jnp.dot(a_low, b_high, preferred_element_type=jnp.float32)
+    return total + jnp.dot(a_high, b_high, preferred_element_type=jnp.float32)
 
 
 def upright(line):
@@ -250,7 +260,7 @@
                     val = val + mine
                 parts.append(weight * val)
             strip = jnp.concatenate(parts, axis=1)
-            out_ref[0, g * step : (g + 1) * step, :] = dot(strip, omega_ref[0], ((1,), (0,)))
+            out_ref[0, g * step : (g + 1) * step, :] = dot_split(strip, omega_ref[0])
 
 
 def col_terms_kernel(ids, left_ref, right_ref, psi_ref, out_ref):
@@ -278,7 +288,7 @@
                     val = val + 1.0
                 parts.append(weight * val)
             strip = jnp.concatenate(parts, axis=1)
-            out_ref[0, p * zones : (p + 1) * zones, :] = dot(strip, psi_ref[0], ((1,), (0,)))
+            out_ref[0, p * zones : (p + 1) * zones, :] = dot_split(strip, psi_ref[0])
 
 
 def add_kernel(row_ids, col_ids, rows_ref, cols_ref, out_rows, out_cols):

time: 224 us -> 220 us (0.982)
  Pallas kernels: 199 us -> 195 us
    pallas_call x1, Pallas kernels: 12.9 us -> 9.88 us  [per_device(): term_call(row_terms_kernel, n_row * slots, height // n_row, lambda n, ids...]
  transfers between devices with their start and end apart: 3 -> 3, of which waited for: 0 -> 0; matrix products, arithmetic and copies ran while one was open for 2% -> 2% of each run, Pallas kernels for 46% -> 45%
where the time goes in v4:
time: 220 us; the launch traced here: 219 us
  Pallas kernels  195 us (89%)
  local copies, waits for them, and re-layouts  10.5 us (5%)
  other arithmetic  7.67 us (3%)
  starting transfers between devices  4.93 us (2%)
    pallas_call x4, Pallas kernels, remote_call(): pl.pallas_call(body, out_shape=out_shapes, in_specs=[ANY] * len(operands)...  141 us
    pallas_call x1, Pallas kernels, per_device(): pl.pallas_call(functools.partial(basis_kernel, own), out_shape=[f32(own,...  35.4 us
    pallas_call x1, Pallas kernels, per_device(): term_call(row_terms_kernel, n_row * slots, height // n_row, lambda n, ids...  9.88 us
    ppermute x3, starting transfers between devices, move_psi(): piece = lax.ppermute(piece, ('row', 'col'), pairs)  4.93 us
  transfers between devices with their start and end apart: 3, of which 0 were waited for; matrix products, arithmetic and copies ran while one was open for 2% of the time, Pallas kernels for 45%

profile of v4, /device:TPU:27, one launch (start us, length us, event | category | flops | bytes accessed | tf_op | source)
XLA Modules:
  0.0 219.1 jit_solution(13135515669248480865)
XLA Ops:
  0.7 0.7 convert_element_type.22
  1.4 0.1 convert_element_type.23
  1.5 1.3 pad_maximum_fusion.points_ref.right_ref
  2.8 0.6 pad.4.meta_ref
  3.4 9.6 %exchange_1.1 = (f32[8,4,1024]{2,1,0:T(4,128)}, f32[12,8,128]{2,1,0:T(8,128)}) custom-call(f32[4,1024]{1,0:T(4,128)} %pad_maximum_fusion.points_ref.right_ref, f32[8,128]{1,0:T(8,128)} %pad.4.meta_ref), custom_call_target="tpu_custom_call" | custom-call | tf_op jit(solution)/shard_map/exchange_1/pallas_call | solution.py:77
  13.0 0.0 copy-start.1
  13.0 3.9 %constant_dynamic-slice_fusion = (f32[2,768,256]{2,1,0:T(8,128)S(1)}, f32[2,768,256]{2,1,0:T(8,128)S(1)}, f32[2,768,256]{2,1,0:T(8,128)}) fusion(f32[16,768,256]{2,1,0:T(8,128)} %psi_ref.1, s32[]{:T(128)S(6)} %select_n.74, s32[]{:T(128)S(6)} %select_n.72, s32[]{:T(128)S(6)} %select_n.70), kind=kLoop, calls=%fused_computation.16 | loop fusion | bytes 9437196 | tf_op jit(solution)/shard_map/dynamic_slice | solution.py:414
  17.0 1.8 collective-permute-start
  18.8 1.3 collective-permute-start.1
  20.1 1.8 collective-permute-start.2
  21.9 0.8 slice_convert_fusion
  22.7 0.1 copy.24
  22.8 0.1 fusion.6
  22.9 0.1 copy.26
  23.0 0.1 stack_reshape_squeeze.4
  23.1 0.7 reshape_squeeze.10.col_ids
  23.7 0.1 copy.27
  23.8 0.1 reshape_squeeze.12
  23.9 0.1 pad.10.clone
  24.0 0.1 copy.25
  24.1 0.6 reshape_squeeze.9.row_ids
  24.7 0.0 copy-done.1
  24.7 0.1 compare_select_fusion
  24.8 0.6 add_add_fusion.1.ids
  25.4 0.7 add_add_fusion.ids
  26.1 4.4 %col_terms.1 = f32[2,768,256]{2,1,0:T(8,128)} custom-call(s32[2,3]{1,0:T(2,128)} %add_add_fusion.1.ids, f32[8,4,1024]{2,1,0:T(4,128)} %get-tuple-element.18.left_ref, f32[4,1024]{1,0:T(4,128)} %pad_maximum_fusion.points_ref.right_ref, f32[16,768,256]{2,1,0:T(8,128)} %psi_ref.1), custom_call_target="tpu_custom_call" | custom-call | flops 3623878656 | bytes 3145728 | tf_op jit(solution)/shard_map/col_terms/pallas_call | solution.py:492
  30.5 9.9 %row_terms.1 = f32[8,192,256]{2,1,0:T(8,128)} custom-call(s32[8,3]{1,0:T(8,128)} %add_add_fusion.ids, f32[8,4,1024]{2,1,0:T(4,128)} %get-tuple-element.18.left_ref, f32[4,1024]{1,0:T(4,128)} %pad_maximum_fusion.points_ref.right_ref, f32[8,768,256]{2,1,0:T(8,128)} %omega_ref.3), custom_call_target="tpu_custom_call" | custom-call | flops 3623878656 | bytes 12582912 | tf_op jit(solution)/shard_map/row_terms/pallas_call | solution.py:484
  40.3 36.7 %exchange_2.1 = (f32[8,2,96,256]{3,2,1,0:T(8,128)}, f32[4,2,192,256]{3,2,1,0:T(8,128)}) custom-call(f32[4,2,192,256]{3,2,1,0:T(8,128)} %bitcast.15, f32[2,768,256]{2,1,0:T(8,128)} %col_terms.1), custom_call_target="tpu_custom_call" | custom-call | tf_op jit(solution)/shard_map/exchange_2/pallas_call | solution.py:77
  77.0 4.3 %sum_terms.1 = (f32[16,96,256]{2,1,0:T(8,128)}, f32[8,192,256]{2,1,0:T(8,128)}) custom-call(s32[16]{0:T(128)} %reshape_squeeze.9.row_ids, s32[8]{0:T(128)} %reshape_squeeze.10.col_ids, f32[8,2,96,256]{3,2,1,0:T(8,128)} %get-tuple-element.19.rows_ref, f32[4,2,192,256]{3,2,1,0:T(8,128)} %get-tuple-element.20.cols_ref), custom_call_target="tpu_custom_call" | custom-call | tf_op jit(solution)/shard_map/sum_terms/pallas_call | solution.py:311
  81.3 43.0 %exchange_3.1 = (f32[8,2,96,256]{3,2,1,0:T(8,128)}, f32[4,2,192,256]{3,2,1,0:T(8,128)}) custom-call(f32[16,96,256]{2,1,0:T(8,128)} %get-tuple-element.21.rows, f32[8,192,256]{2,1,0:T(8,128)} %get-tuple-element.22.cols), custom_call_target="tpu_custom_call" | custom-call | tf_op jit(solution)/shard_map/exchange_3/pallas_call | solution.py:77
  124.3 0.0 collective-permute-done
  124.3 0.0 collective-permute-done.1
  124.3 0.0 collective-permute-done.2
  124.3 3.4 %select_select_fusion.psi_ref = f32[2,768,256]{2,1,0:T(8,128)} fusion(f32[2,768,256]{2,1,0:T(8,128)} %collective-permute-done, f32[2,768,256]{2,1,0:T(8,128)} %collective-permute-done.1, f32[2,768,256]{2,1,0:T(8,128)} %collective-permute-done.2, f32[16,768,256]{2,1,0:T(8,128)} %psi_ref.1, s32[]{:T(128)S(6)} %select_n.75, pred[]{:T(512)S(6)} %eq.11, ...), kind=kLoop, calls=%fused_computation | loop fusion | flops 1179648 | bytes 7864327 | tf_op jit(solution)/shard_map/jit(_where)/select_n | solution.py:420
  127.8 35.4 %basis.1 = (f32[2,768,256]{2,1,0:T(8,128)}, f32[2,768,256]{2,1,0:T(8,128)}) custom-call(s32[1]{0:T(128)} %bitcast.place, f32[8,2,96,256]{3,2,1,0:T(8,128)} %get-tuple-element.23.row_terms, f32[4,2,192,256]{3,2,1,0:T(8,128)} %get-tuple-element.24.col_terms, f32[8,768,256]{2,1,0:T(8,128)} %omega_ref.3, f32[2,768,256]{2,1,0:T(8,128)} %select_select_fusion.psi_ref, ...), custom_call_target="tpu_custom_call" | custom-call | tf_op jit(solution)/shard_map/basis/pallas_call | solution.py:525
  163.2 52.0 %exchange_4.1 = (f32[16,96,256]{2,1,0:T(8,128)}, f32[8,192,256]{2,1,0:T(8,128)}) custom-call(f32[2,768,256]{2,1,0:T(8,128)} %get-tuple-element.26.rows, f32[2,768,256]{2,1,0:T(8,128)} %get-tuple-element.27.cols), custom_call_target="tpu_custom_call" | custom-call | tf_op jit(solution)/shard_map/exchange_4/pallas_call | solution.py:77
  215.2 0.0 copy-start
  215.2 2.8 %copy.34 = f32[16,96,256]{2,1,0:T(8,128)} copy(f32[16,96,256]{2,1,0:T(8,128)} %get-tuple-element.37) | data formatting | bytes 3145728
  218.0 0.0 copy-done
  218.0 1.1 copy.35
  (2 shorter events, 0.0 us)
Async XLA Ops:
  13.0 11.7 %copy-start.1 = (s32[1,1,2,2]{3,2,1,0:T(2,128)S(1)}, s32[1,1,2,2]{3,2,1,0:T(2,128)}, u32[]{:S(2)}) copy-start(s32[1,1,2,2]{3,2,1,0:T(2,128)} %param.11) | copy-start | bytes 52
  17.0 107.3 %collective-permute-start = (f32[2,768,256]{2,1,0:T(8,128)}, f32[2,768,256]{2,1,0:T(8,128)}, u32[]{:S(2)}, u32[]{:S(2)}) collective-permute-start(f32[2,768,256]{2,1,0:T(8,128)} %get-tuple-element.30), channel_id=1, source_target_pairs={{0,24},{1,25},{10,2},{11,3},{20,12},{21,13},{30,22},{31,23}} | collective-permute-start | bytes 4718600 | tf_op jit(solution)/shard_map/ppermute | solution.py:419
  18.8 105.5 %collective-permute-start.1 = (f32[2,768,256]{2,1,0:T(8,128)S(1)}, f32[2,768,256]{2,1,0:T(8,128)}, u32[]{:S(2)}, u32[]{:S(2)}) collective-permute-start(f32[2,768,256]{2,1,0:T(8,128)S(1)} %get-tuple-element.29), channel_id=1, source_target_pairs={{0,16},{1,17},{10,26},{11,27},{20,4},{21,5},{30,14},{31,15}} | collective-permute-start | bytes 4718600 | tf_op jit(solution)/shard_map/ppermute | solution.py:419
  20.1 104.3 %collective-permute-start.2 = (f32[2,768,256]{2,1,0:T(8,128)S(1)}, f32[2,768,256]{2,1,0:T(8,128)}, u32[]{:S(2)}, u32[]{:S(2)}) collective-permute-start(f32[2,768,256]{2,1,0:T(8,128)S(1)} %get-tuple-element.28), channel_id=1, source_target_pairs={{0,8},{1,9},{10,18},{11,19},{20,28},{21,29},{30,6},{31,7}} | collective-permute-start | bytes 4718600 | tf_op jit(solution)/shard_map/ppermute | solution.py:419
  215.2 2.8 %copy-start = (f32[8,192,256]{2,1,0:T(8,128)S(1)}, f32[8,192,256]{2,1,0:T(8,128)}, u32[]{:S(2)}) copy-start(f32[8,192,256]{2,1,0:T(8,128)} %get-tuple-element.38) | copy-start | bytes 4718596
